TPU v7x, 256 devices: a whole 4x4x8 slice. The times are simulated.
256 devices in a mesh: gx: 8 (over y, core), gy: 32 (over x, z).
Axes of the slice: x: 4, y: 4, z: 8, core: 2. Of those that a mesh axis runs over, the one named last changes fastest.
Arguments:
- features: bfloat16 [8, 32, 2, 512, 128], P('gx', 'gy'), may hold values from -6 to 6
- grad_out: bfloat16 [8, 32, 2, 512, 128], P('gx', 'gy'), may hold values from -6 to 6
- weight: bfloat16 [27, 128, 128], replicated, may hold values from -0.109375 to 0.109375
- neighbours: int32 [8, 32, 2, 27], P('gx', 'gy'), may hold values from -1 to 17, as said below
Outputs:
- out_features: bfloat16 [8, 32, 2, 512, 128], P('gx', 'gy')
- grad_features: bfloat16 [8, 32, 2, 512, 128], P('gx', 'gy')
- grad_weight: float32 [27, 128, 128], replicated
Inputs may be any that keep to these rules, and one draw needn't show every extreme that they name: neighbours[i, j, s, k] is (3 * (di + 1) + (dj + 1)) * 2 + t when the block at offset k from slot s of region (i, j) is active and sits in slot t of region (i + di, j + dj), with di and dj in -1, 0, 1; else -1. Blocks lie on a scene of 16 x 64 x 1 positions, region (i, j) owning x positions 2i, 2i + 1 and y positions 2j, 2j + 1; the relation is symmetric. Each region has 1 to 2 active slots, its first ones, and some region has all 2; an inactive slot has -1 in every entry and its features and grad_out are never read.
All inputs are finite; a program needn't handle non-finite values.
Results may differ from a plain program's by a relative error of at most 0.001.
Values may be sent and summed in bfloat16 or wider, within the bound.
A program may use at most 64 MiB of HBM per device.

v0:
```python
import math

import jax
import jax.numpy as jnp
from jax import lax
from jax.sharding import PartitionSpec as P

BLK = 8


def with_halo(block, sides, width):
    for axis, dim in sides:
        count = lax.axis_size(axis)
        forward = [(i, i + 1) for i in range(count - 1)]
        backward = [(target, source) for source, target in forward]
        low = lax.ppermute(
            lax.slice_in_dim(block, block.shape[dim] - width, None, axis=dim), axis, forward
        )
        high = lax.ppermute(lax.slice_in_dim(block, 0, width, axis=dim), axis, backward)
        block = jnp.concatenate([low, block, high], axis=dim)
    return block


def assemble(block_pool, neighbour_ids, block_edge):
    slot_count = neighbour_ids.shape[0]
    channels = block_pool.shape[-1]
    ranges = ((block_edge - 1, block_edge), (0, block_edge), (0, 1))
    planes = []
    for a in range(3):
        row_list = []
        for b in range(3):
            columns = []
            for c in range(3):
                chosen_ids = neighbour_ids[:, (a * 3 + b) * 3 + c]
                picked = jnp.take(block_pool, jnp.maximum(chosen_ids, 0), axis=0)
                picked = jnp.where(
                    (chosen_ids >= 0)[:, None, None], picked, jnp.zeros((), block_pool.dtype)
                )
                portion = picked.reshape(slot_count, block_edge, block_edge, block_edge, channels)
                portion = portion[
                    :,
                    ranges[a][0] : ranges[a][1],
                    ranges[b][0] : ranges[b][1],
                    ranges[c][0] : ranges[c][1],
                    :,
                ]
                columns.append(portion)
            row_list.append(jnp.concatenate(columns, axis=3))
        planes.append(jnp.concatenate(row_list, axis=2))
    return jnp.concatenate(planes, axis=1)


def local_pass(pool_feat, pool_grad, own_grad, neighbour_ids, weight, block_edge):
    channels = weight.shape[-1]
    padded_feat = assemble(pool_feat, neighbour_ids, block_edge)
    padded_grad = assemble(pool_grad, neighbour_ids, block_edge)
    grad_flat = own_grad.reshape(-1, channels)
    running_out = None
    running_in = None
    partial_value = []
    for a in range(3):
        for b in range(3):
            for c in range(3):
                k = (a * 3 + b) * 3 + c
                window = padded_feat[
                    :, a : a + block_edge, b : b + block_edge, c : c + block_edge, :
                ].reshape(-1, channels)
                term_out = jnp.dot(window, weight[k], preferred_element_type=jnp.float32)
                running_out = term_out if running_out is None else running_out + term_out
                partial_value.append(
                    lax.dot_general(
                        window,
                        grad_flat,
                        (((0,), (0,)), ((), ())),
                        preferred_element_type=jnp.float32,
                    )
                )
                back_window = padded_grad[
                    :,
                    2 - a : 2 - a + block_edge,
                    2 - b : 2 - b + block_edge,
                    2 - c : 2 - c + block_edge,
                    :,
                ].reshape(-1, channels)
                term_in = lax.dot_general(
                    back_window,
                    weight[k],
                    (((1,), (1,)), ((), ())),
                    preferred_element_type=jnp.float32,
                )
                running_in = term_in if running_in is None else running_in + term_in
    return (
        running_out.astype(jnp.bfloat16),
        running_in.astype(jnp.bfloat16),
        jnp.stack(partial_value),
    )


def local(features, grad_out, weight, neighbours):
    slot_count = features.shape[2]
    voxels = features.shape[3]
    channels = features.shape[4]
    stacked = jnp.stack([features, grad_out])
    extended = with_halo(stacked, (("gx", 1), ("gy", 2)), 1)
    pool_feat = extended[0].reshape(9 * slot_count, voxels, channels)
    pool_grad = extended[1].reshape(9 * slot_count, voxels, channels)
    neighbour_ids = neighbours.reshape(slot_count, 27)
    output, grad_in, partial_value = local_pass(
        pool_feat, pool_grad, grad_out, neighbour_ids, weight, BLK
    )
    summed = lax.psum(partial_value, ("gx", "gy"))
    total_slots = lax.axis_size("gx") * lax.axis_size("gy") * slot_count * voxels
    scale_factor = 1.0 / math.sqrt(total_slots)
    return (output.reshape(features.shape), grad_in.reshape(features.shape), summed * scale_factor)


def solution(mesh):
    in_specs = (
        P("gx", "gy", None, None, None),
        P("gx", "gy", None, None, None),
        P(),
        P("gx", "gy", None, None),
    )
    out_specs = (P("gx", "gy", None, None, None), P("gx", "gy", None, None, None), P())
    return jax.shard_map(local, mesh=mesh, in_specs=in_specs, out_specs=out_specs, check_vma=False)
```

profile of v0, /device:TPU:15, one launch (start us, length us, event | category | flops | bytes accessed | tf_op | source)
XLA Modules:
  0.0 519.5 jit_solution(4606748040905097856)
XLA Ops:
  8.4 2.6 collective-permute-start.1
  10.9 3.1 collective-permute-start
  18.4 1.9 compare_reduce_fusion.8
  20.3 1.9 maximum_reduce_fusion.8
  24.1 7.8 %collective-permute-start.3 = (bf16[2,3,1,2,512,128]{5,4,3,2,1,0:T(8,128)(2,1)S(1)}, bf16[2,3,1,2,512,128]{5,4,3,2,1,0:T(8,128)(2,1)S(1)}, u32[]{:S(2)}, u32[]{:S(2)}) collective-permute-start(bf16[2,3,1,2,512,128]{5,4,3,2,1,0:T(8,128)(2,1)S(1)} %pad_maximum_fusion.1), channel_id=1, source_target_pairs={{1,0},{2,1},{3,2},{4,3},{5,4},{6,5},{7,6},{8,7},{9,8},{10,9},{11,1... | collective-permute-start | bytes 4718600 | tf_op jit(solution)/shard_map/ppermute | solution.py:19
  31.8 2.1 collective-permute-start.2
  37.4 28.4 %collective-permute-done.3 = bf16[2,3,1,2,512,128]{5,4,3,2,1,0:T(8,128)(2,1)S(1)} collective-permute-done((bf16[2,3,1,2,512,128]{5,4,3,2,1,0:T(8,128)(2,1)S(1)}, bf16[2,3,1,2,512,128]{5,4,3,2,1,0:T(8,128)(2,1)S(1)}, u32[]{:S(2)}, u32[]{:S(2)}) %collective-permute-start.3) | collective-permute-done | bytes 1572896 | tf_op jit(solution)/shard_map/ppermute | solution.py:19
  65.8 6.4 %collective-permute-done.2 = bf16[2,3,1,2,512,128]{5,4,3,2,1,0:T(8,128)(2,1)S(1)} collective-permute-done((bf16[2,3,1,2,512,128]{5,4,3,2,1,0:T(8,128)(2,1)S(1)}, bf16[2,3,1,2,512,128]{5,4,3,2,1,0:T(8,128)(2,1)S(1)}, u32[]{:S(2)}, u32[]{:S(2)}) %collective-permute-start.2) | collective-permute-done | bytes 1572896 | tf_op jit(solution)/shard_map/ppermute | solution.py:16
  72.8 1.7 fusion.139
  74.6 3.0 gather_fusion.26
  78.8 2.9 gather_fusion.25
  81.7 1.3 gather_fusion.43
  83.0 2.9 gather_fusion.24
  87.2 3.0 gather_fusion.23
  91.5 3.0 gather_fusion.22
  95.7 3.0 gather_fusion.21
  98.7 1.3 gather_fusion.39
  100.0 3.0 gather_fusion.20
  102.9 1.3 gather_fusion.38
  104.2 2.9 gather_fusion.19
  108.4 2.9 gather_fusion.18
  112.7 2.9 gather_fusion.17
  116.9 3.0 gather_fusion.16
  121.1 2.9 gather_fusion.15
  124.1 1.3 gather_fusion.33
  125.4 3.0 gather_fusion.14
  129.6 2.3 gather_fusion.13
  132.5 3.0 gather_fusion.12
  135.5 1.3 gather_fusion.30
  136.7 2.9 gather_fusion.11
  141.0 2.9 gather_fusion.10
  145.2 3.0 gather_fusion.9
  149.4 2.9 gather_fusion.8
  153.7 3.0 gather_fusion.7
  156.6 1.3 gather_fusion.52
  157.9 3.0 gather_fusion.6
  160.9 1.3 gather_fusion.51
  162.2 3.0 gather_fusion.5
  166.4 2.9 gather_fusion.4
  170.6 3.0 gather_fusion.3
  173.6 1.3 gather_fusion.48
  174.9 2.9 gather_fusion.2
  179.1 2.9 gather_fusion
  183.3 2.3 gather_fusion.1
  203.9 1.4 fusion.141
  207.2 1.5 fusion.140
  264.7 245.1 %all-reduce.2.cloned.1.call-done = f32[27,128,128]{2,1,0:T(8,128)} async-done(((f32[27,128,128]{2,1,0:T(8,128)}), f32[27,128,128]{2,1,0:T(8,128)}) %all-reduce.2.cloned.1.call-update) | async-done | bytes 1769488 | tf_op jit(solution)/shard_map/psum | solution.py:111
  509.7 2.9 broadcast_multiply_fusion
  (431 shorter events, 108.1 us)
Async XLA Ops:
  7.2 16.7 %copy-start = (bf16[1,1,2,512,128]{4,3,2,1,0:T(8,128)(2,1)S(1)}, bf16[1,1,2,512,128]{4,3,2,1,0:T(8,128)(2,1)}, u32[]{:S(2)}) copy-start(bf16[1,1,2,512,128]{4,3,2,1,0:T(8,128)(2,1)} %param.7) | copy-start | bytes 786436
  7.2 16.7 %copy-start.2 = (bf16[1,1,2,512,128]{4,3,2,1,0:T(8,128)(2,1)S(1)}, bf16[1,1,2,512,128]{4,3,2,1,0:T(8,128)(2,1)}, u32[]{:S(2)}) copy-start(bf16[1,1,2,512,128]{4,3,2,1,0:T(8,128)(2,1)} %param.6) | copy-start | bytes 786436
  7.2 502.6 %all-reduce.2.cloned.1.call-start = ((), (), s32[]{:S(2)}) async-start(), calls=%async_computation | async-start | bytes 3538944 | tf_op jit(solution)/shard_map/psum | solution.py:111
  8.4 15.5 %collective-permute-start.1 = (bf16[2,1,1,2,512,128]{5,4,3,2,1,0:T(8,128)(2,1)S(1)}, bf16[2,1,1,2,512,128]{5,4,3,2,1,0:T(8,128)(2,1)S(1)}, u32[]{:S(2)}, u32[]{:S(2)}) collective-permute-start(bf16[2,1,1,2,512,128]{5,4,3,2,1,0:T(8,128)(2,1)S(1)} %pad_maximum_fusion.2), channel_id=1, source_target_pairs={{32,0},{64,32},{96,64},{128,96},{160,128},{192,160},{224,192},{33,... | collective-permute-start | bytes 1572872 | tf_op jit(solution)/shard_map/ppermute | solution.py:19
  10.9 12.9 %collective-permute-start = (bf16[2,1,1,2,512,128]{5,4,3,2,1,0:T(8,128)(2,1)S(1)}, bf16[2,1,1,2,512,128]{5,4,3,2,1,0:T(8,128)(2,1)S(1)}, u32[]{:S(2)}, u32[]{:S(2)}) collective-permute-start(bf16[2,1,1,2,512,128]{5,4,3,2,1,0:T(8,128)(2,1)S(1)} %pad_maximum_fusion.2), channel_id=1, source_target_pairs={{0,32},{32,64},{64,96},{96,128},{128,160},{160,192},{192,224},{1,3... | collective-permute-start | bytes 1572872 | tf_op jit(solution)/shard_map/ppermute | solution.py:16
  24.1 41.7 %collective-permute-start.3 = (bf16[2,3,1,2,512,128]{5,4,3,2,1,0:T(8,128)(2,1)S(1)}, bf16[2,3,1,2,512,128]{5,4,3,2,1,0:T(8,128)(2,1)S(1)}, u32[]{:S(2)}, u32[]{:S(2)}) collective-permute-start(bf16[2,3,1,2,512,128]{5,4,3,2,1,0:T(8,128)(2,1)S(1)} %pad_maximum_fusion.1), channel_id=1, source_target_pairs={{1,0},{2,1},{3,2},{4,3},{5,4},{6,5},{7,6},{8,7},{9,8},{10,9},{11,1... | collective-permute-start | bytes 4718600 | tf_op jit(solution)/shard_map/ppermute | solution.py:19
  31.8 40.4 %collective-permute-start.2 = (bf16[2,3,1,2,512,128]{5,4,3,2,1,0:T(8,128)(2,1)S(1)}, bf16[2,3,1,2,512,128]{5,4,3,2,1,0:T(8,128)(2,1)S(1)}, u32[]{:S(2)}, u32[]{:S(2)}) collective-permute-start(bf16[2,3,1,2,512,128]{5,4,3,2,1,0:T(8,128)(2,1)S(1)} %pad_maximum_fusion.1), channel_id=1, source_target_pairs={{0,1},{1,2},{2,3},{3,4},{4,5},{5,6},{6,7},{7,8},{8,9},{9,10},{10,1... | collective-permute-start | bytes 4718600 | tf_op jit(solution)/shard_map/ppermute | solution.py:16
  186.9 2.6 copy-start.48
  186.9 2.6 copy-start.49
  186.9 3.5 copy-start.46
  186.9 3.5 copy-start.47
  186.9 3.5 copy-start.74
  188.2 2.4 copy-start.44
  188.2 2.4 copy-start.45
  188.2 2.4 copy-start.72
  189.4 1.3 copy-start.42
  189.5 1.3 copy-start.43
  190.8 1.1 copy-start.37
  190.8 1.1 copy-start.82
  191.4 1.1 copy-start.35
  191.4 1.1 copy-start.81
  191.7 1.1 copy-start.33
  191.7 1.1 copy-start.85
  191.9 1.1 copy-start.31
  191.9 1.1 copy-start.84
  192.5 1.1 copy-start.29
  192.5 1.1 copy-start.83
  193.2 1.2 copy-start.24
  193.2 1.2 copy-start.25
  193.2 1.2 copy-start.79
  193.8 1.1 copy-start.23
  194.4 1.1 copy-start.19
  194.9 1.1 copy-start.17
  194.9 1.1 copy-start.75
  195.2 1.1 copy-start.15
  195.2 1.1 copy-start.73
  195.5 1.1 copy-start.13
  195.5 1.1 copy-start.71
  196.0 1.1 copy-start.11
  196.3 1.1 copy-start.9
  196.6 1.1 copy-start.7
  197.1 1.1 copy-start.5
  197.1 1.1 copy-start.86
  209.2 1.2 copy-start.1
  252.8 1.3 copy-start.64
  252.8 1.5 copy-start.63
  262.0 1.2 copy-start.51
  262.3 1.2 copy-start.50
  (44 other events, 44.9 us)
Sparse Core Ops, SparseCore 0:
  252.9 256.7 all-reduce.1
where the time goes:
time: 524 us; the launch traced here: 519 us
  waiting for transfers between devices  280 us (53%)
  local copies, waits for them, and re-layouts  128 us (24%)
  matrix products  50.6 us (10%)
  other arithmetic  28.9 us (6%)
  between operations  16.1 us (3%)
  starting transfers between devices  15.6 us (3%)
    psum x1, waiting for transfers between devices, local(): summed = lax.psum(partial_value, ('gx', 'gy'))  245 us
    gather x54, local copies, waits for them, and re-layouts, assemble(): picked = jnp.take(block_pool, jnp.maximum(chosen_ids, 0), axis=0)  112 us
    ppermute x2, waiting for transfers between devices, with_halo(): lax.ppermute(lax.slice_in_dim(block, 0, width, axis=dim), axis, backward)  28.4 us
    dot_general x27, matrix products, local_pass(): lax.dot_general(window, grad_flat, (((0,), (0,)), ((), ())), preferred_el...  24.5 us
    dot_general x27, matrix products, local_pass(): term_out = jnp.dot(window, weight[k], preferred_element_type=jnp.float32)  18.4 us
  transfers between devices with their start and end apart: 5, of which 3 were waited for; matrix products, arithmetic and copies ran while one was open for 4% of the time, Pallas kernels for 0%

commit v1 on v0

v1 whole, which is shorter than its diff:
```python
import math

import jax
import jax.numpy as jnp
from jax import lax
from jax.sharding import PartitionSpec as P

BLK = 8


def shift(x, axes, step):
    sizes = [lax.axis_size(a) for a in axes]
    pairs = []
    for src in range(math.prod(sizes)):
        coords, rest = [], src
        for size in reversed(sizes):
            coords.append(rest % size)
            rest //= size
        coords = coords[::-1]
        dst = [c + d for c, d in zip(coords, step)]
        if all(0 <= c < s for c, s in zip(dst, sizes)):
            flat = 0
            for c, s in zip(dst, sizes):
                flat = flat * s + c
            pairs.append((src, flat))
    return lax.ppermute(x, axes if len(axes) > 1 else axes[0], pairs)


def neighbour_pool(both):
    x7, x0 = both[:, :, 7], both[:, :, 0]
    y7, y0 = both[:, :, :, 7], both[:, :, :, 0]
    zero = jnp.zeros_like(both)
    recv = {
        (-1, 0): zero.at[:, :, 7].set(shift(x7, ("gx",), (1,))),
        (1, 0): zero.at[:, :, 0].set(shift(x0, ("gx",), (-1,))),
        (0, -1): zero.at[:, :, :, 7].set(shift(y7, ("gy",), (1,))),
        (0, 1): zero.at[:, :, :, 0].set(shift(y0, ("gy",), (-1,))),
        (-1, -1): zero.at[:, :, 7, 7].set(shift(both[:, :, 7, 7], ("gx", "gy"), (1, 1))),
        (-1, 1): zero.at[:, :, 7, 0].set(shift(both[:, :, 7, 0], ("gx", "gy"), (1, -1))),
        (1, -1): zero.at[:, :, 0, 7].set(shift(both[:, :, 0, 7], ("gx", "gy"), (-1, 1))),
        (1, 1): zero.at[:, :, 0, 0].set(shift(both[:, :, 0, 0], ("gx", "gy"), (-1, -1))),
        (0, 0): both,
    }
    blocks = [recv[(di, dj)] for di in (-1, 0, 1) for dj in (-1, 0, 1)]
    pool = jnp.stack(blocks, axis=1)
    return pool.reshape(2, 9 * both.shape[1], -1)


def assemble(picked, block_edge):
    ranges = ((block_edge - 1, block_edge), (0, block_edge), (0, 1))
    planes = []
    for a in range(3):
        row_list = []
        for b in range(3):
            columns = []
            for c in range(3):
                k = (a * 3 + b) * 3 + c
                portion = picked[
                    :,
                    k,
                    :,
                    ranges[a][0] : ranges[a][1],
                    ranges[b][0] : ranges[b][1],
                    ranges[c][0] : ranges[c][1],
                    :,
                ]
                columns.append(portion)
            row_list.append(jnp.concatenate(columns, axis=4))
        planes.append(jnp.concatenate(row_list, axis=3))
    cube = jnp.concatenate(planes, axis=2)
    return jnp.swapaxes(cube, 0, 1)


def im2col(cube, block_edge):
    windows = []
    for a in range(3):
        for b in range(3):
            for c in range(3):
                windows.append(
                    cube[:, a : a + block_edge, b : b + block_edge, c : c + block_edge, :]
                )
    cols = jnp.concatenate(windows, axis=-1)
    return cols.reshape(-1, cols.shape[-1])


def butterfly_sum(x, axes):
    n = math.prod(lax.axis_size(a) for a in axes)
    bits = n.bit_length() - 1
    flat = x.reshape(-1)
    me = lax.axis_index(axes)
    gx_bits = int(math.log2(lax.axis_size(axes[0])))
    gy_bits = bits - gx_bits
    order = [gy_bits + i for i in range(gx_bits)] + list(range(gy_bits))
    order = [order[0]] + sorted(order[1:], key=lambda b: (b % 3, b))
    pairs = lambda b: [(j, j ^ (1 << b)) for j in range(n)]
    for b in order:
        half = flat.shape[0] // 2
        bit = (me >> b) & 1
        keep = lax.dynamic_slice(flat, (bit * half,), (half,))
        send = lax.dynamic_slice(flat, ((1 - bit) * half,), (half,))
        flat = keep + lax.ppermute(send, axes, pairs(b))
    for b in reversed(order):
        bit = (me >> b) & 1
        other = lax.ppermute(flat, axes, pairs(b))
        flat = jnp.where(
            bit == 0, jnp.concatenate([flat, other]), jnp.concatenate([other, flat])
        )
    return flat.reshape(x.shape)


def local(features, grad_out, weight, neighbours):
    slot_count = features.shape[2]
    voxels = features.shape[3]
    channels = features.shape[4]
    e = BLK
    both = jnp.stack([features[0, 0], grad_out[0, 0]]).reshape(
        2, slot_count, e, e, e, channels
    )
    pool = neighbour_pool(both)
    ids = neighbours.reshape(slot_count * 27)
    onehot = (ids[:, None] == jnp.arange(pool.shape[1])[None, :]).astype(pool.dtype)
    picked = jnp.einsum(
        "mn,anf->maf", onehot, pool, preferred_element_type=jnp.float32
    ).astype(pool.dtype)
    picked = picked.reshape(slot_count, 27, 2, e, e, e, channels)
    cubes = assemble(picked, e)
    cols_feat = im2col(cubes[0], e)
    cols_grad = im2col(cubes[1], e)
    grad_flat = grad_out.reshape(-1, channels)
    partial_value = lax.dot_general(
        cols_feat, grad_flat, (((0,), (0,)), ((), ())), preferred_element_type=jnp.float32
    ).reshape(27, channels, channels)
    summed = butterfly_sum(partial_value, ("gx", "gy"))
    w_out = weight.reshape(27 * channels, channels)
    w_in = jnp.swapaxes(weight[::-1], 1, 2).reshape(27 * channels, channels)
    output = jnp.dot(cols_feat, w_out, preferred_element_type=jnp.float32)
    grad_in = jnp.dot(cols_grad, w_in, preferred_element_type=jnp.float32)
    total_slots = lax.axis_size("gx") * lax.axis_size("gy") * slot_count * voxels
    scale_factor = 1.0 / math.sqrt(total_slots)
    return (
        output.astype(jnp.bfloat16).reshape(features.shape),
        grad_in.astype(jnp.bfloat16).reshape(features.shape),
        summed * scale_factor,
    )


def solution(mesh):
    in_specs = (
        P("gx", "gy", None, None, None),
        P("gx", "gy", None, None, None),
        P(),
        P("gx", "gy", None, None),
    )
    out_specs = (P("gx", "gy", None, None, None), P("gx", "gy", None, None, None), P())
    return jax.shard_map(local, mesh=mesh, in_specs=in_specs, out_specs=out_specs, check_vma=False)
```

time: 524 us -> 212 us (0.40)
  waiting for transfers between devices: 280 us -> 62.3 us
  local copies, waits for them, and re-layouts: 128 us -> 57.7 us
  starting transfers between devices: 15.6 us -> 54.9 us
  matrix products: 50.6 us -> 24 us
  other arithmetic: 28.9 us -> 9.95 us
  between operations: 16.1 us -> 1.57 us
    psum x1 -> x0, waiting for transfers between devices: 245 us -> none  [local(): summed = lax.psum(partial_value, ('gx', 'gy'))]
    gather x54 -> x0, local copies, waits for them, and re-layouts: 112 us -> none  [assemble(): picked = jnp.take(block_pool, jnp.maximum(chosen_ids, 0), axis=0)]
    ppermute x4 -> x24, starting transfers between devices: 15.5 us -> 54.9 us  [the longest x8 27.4 us: shift(): return lax.ppermute(x, axes if len(axes) > 1 else axes[0], pairs)]
    reshape x0 -> x2, local copies, waits for them, and re-layouts: none -> 31.6 us  [the longest x1 19.9 us: local(): picked = picked.reshape(slot_count, 27, 2, e, e, e, channels)]
    ppermute x4 -> x24, waiting for transfers between devices: 34.7 us -> 62.3 us  [the longest x8 34.5 us: butterfly_sum(): flat = keep + lax.ppermute(send, axes, pairs(b))]
    dot_general x81 -> x4, matrix products: 50.6 us -> 24 us  [the longest x1 16.5 us: local(): jnp.einsum('mn,anf->maf', onehot, pool, preferred_element_type=jnp.float32)]
    unnamed x174 -> x74, local copies, waits for them, and re-layouts: 7.65 us -> 14.3 us
    and x14 -> x0, other arithmetic: 6.44 us -> none  [assemble(): picked = jnp.take(block_pool, jnp.maximum(chosen_ids, 0), axis=0)]
  transfers between devices with their start and end apart: 5 -> 24, of which waited for: 3 -> 16; matrix products, arithmetic and copies ran while one was open for 4% -> 12% of each run, Pallas kernels for 0% -> 0%
where the time goes in v1:
time: 212 us; the launch traced here: 210 us
  waiting for transfers between devices  62.3 us (29%)
  local copies, waits for them, and re-layouts  57.7 us (27%)
  starting transfers between devices  54.9 us (26%)
  matrix products  24 us (11%)
  other arithmetic  9.95 us (5%)
    ppermute x8, waiting for transfers between devices, butterfly_sum(): flat = keep + lax.ppermute(send, axes, pairs(b))  34.5 us
    ppermute x8, starting transfers between devices, shift(): return lax.ppermute(x, axes if len(axes) > 1 else axes[0], pairs)  27.4 us
    ppermute x8, waiting for transfers between devices, butterfly_sum(): other = lax.ppermute(flat, axes, pairs(b))  26.1 us
    ppermute x8, starting transfers between devices, butterfly_sum(): other = lax.ppermute(flat, axes, pairs(b))  20.5 us
    reshape x1, local copies, waits for them, and re-layouts, local(): picked = picked.reshape(slot_count, 27, 2, e, e, e, channels)  19.9 us
    dot_general x1, matrix products, local(): jnp.einsum('mn,anf->maf', onehot, pool, preferred_element_type=jnp.float32)  16.5 us
    unnamed x74, local copies, waits for them, and re-layouts  14.3 us
    reshape x1, local copies, waits for them, and re-layouts, neighbour_pool(): return pool.reshape(2, 9 * both.shape[1], -1)  11.6 us
  transfers between devices with their start and end apart: 24, of which 16 were waited for; matrix products, arithmetic and copies ran while one was open for 12% of the time, Pallas kernels for 0%

profile of v1, /device:TPU:15, one launch (start us, length us, event | category | flops | bytes accessed | tf_op | source)
XLA Modules:
  0.0 210.4 jit_solution(13834962362461635018)
XLA Ops:
  1.5 5.1 %collective-permute-start = (bf16[2,2,8,128]{3,2,0,1:T(8,128)(2,1)S(1)}, bf16[2,2,8,128]{3,2,0,1:T(8,128)(2,1)S(1)}, u32[]{:S(2)}, u32[]{:S(2)}) collective-permute-start(bf16[2,2,8,128]{3,2,0,1:T(8,128)(2,1)S(1)} %bitcast.187), channel_id=1, source_target_pairs={{0,33},{1,34},{2,35},{3,36},{4,37},{5,38},{6,39},{7,40},{8,41},{9,... | collective-permute-start | bytes 24584 | tf_op jit(solution)/shard_map/ppermute | solution.py:26
  7.5 1.9 collective-permute-start.1
  9.4 6.1 %collective-permute-start.2 = (bf16[2,2,8,128]{3,2,0,1:T(8,128)(2,1)S(1)}, bf16[2,2,8,128]{3,2,0,1:T(8,128)(2,1)S(1)}, u32[]{:S(2)}, u32[]{:S(2)}) collective-permute-start(bf16[2,2,8,128]{3,2,0,1:T(8,128)(2,1)S(1)} %bitcast.186), channel_id=1, source_target_pairs={{1,32},{2,33},{3,34},{4,35},{5,36},{6,37},{7,38},{8,39},{9,40},{10... | collective-permute-start | bytes 24584 | tf_op jit(solution)/shard_map/ppermute | solution.py:26
  16.4 1.9 collective-permute-start.3
  18.4 1.9 collective-permute-start.5
  20.4 1.3 and_reduce_fusion
  23.1 1.9 copy.98
  25.0 1.7 collective-permute-done.5
  26.7 4.4 %collective-permute-start.4 = (bf16[2,2,8,8,128]{4,3,0,1,2:T(8,128)(2,1)S(1)}, bf16[2,2,8,8,128]{4,3,0,1,2:T(8,128)(2,1)S(1)}, u32[]{:S(2)}, u32[]{:S(2)}) collective-permute-start(bf16[2,2,8,8,128]{4,3,0,1,2:T(8,128)(2,1)S(1)} %bitcast.181), channel_id=1, source_target_pairs={{1,0},{2,1},{3,2},{4,3},{5,4},{6,5},{7,6},{8,7},{9,8},{10,9},{11,1... | collective-permute-start | bytes 196616 | tf_op jit(solution)/shard_map/ppermute | solution.py:26
  31.2 2.0 bitcast_dynamic-update-slice_fusion
  33.2 2.6 %collective-permute-start.6 = (bf16[2,2,8,8,128]{4,3,0,1,2:T(8,128)(2,1)S(1)}, bf16[2,2,8,8,128]{4,3,0,1,2:T(8,128)(2,1)S(1)}, u32[]{:S(2)}, u32[]{:S(2)}) collective-permute-start(bf16[2,2,8,8,128]{4,3,0,1,2:T(8,128)(2,1)S(1)} %bitcast.180), channel_id=1, source_target_pairs={{32,0},{64,32},{96,64},{128,96},{160,128},{192,160},{224,192},{33,... | collective-permute-start | bytes 196616 | tf_op jit(solution)/shard_map/ppermute | solution.py:26
  36.7 3.4 %collective-permute-start.7 = (bf16[2,2,8,128]{3,2,0,1:T(8,128)(2,1)S(1)}, bf16[2,2,8,128]{3,2,0,1:T(8,128)(2,1)S(1)}, u32[]{:S(2)}, u32[]{:S(2)}) collective-permute-start(bf16[2,2,8,128]{3,2,0,1:T(8,128)(2,1)S(1)} %bitcast.189), channel_id=1, source_target_pairs={{33,0},{34,1},{35,2},{36,3},{37,4},{38,5},{39,6},{40,7},{41,8},{42... | collective-permute-start | bytes 24584 | tf_op jit(solution)/shard_map/ppermute | solution.py:26
  40.1 0.9 pad_dynamic-update-slice_fusion.4
  43.7 0.9 pad_dynamic-update-slice_fusion.1
  47.3 11.6 %reshape.441 = bf16[2,18,65536]{2,0,1:T(2,128)(2,1)} reshape(bf16[2,9,2,8,8,8,128]{6,5,4,3,0,2,1:T(8,128)(2,1)} %pad_dynamic-update-slice_fusion.6) | data formatting | bytes 9437184 | tf_op jit(solution)/shard_map/reshape | solution.py:46
  58.9 16.5 %convolution_convert_fusion = bf16[54,2,65536]{2,0,1:T(8,128)(2,1)} fusion(bf16[2,18,65536]{2,0,1:T(2,128)(2,1)} %reshape.441, s32[54]{0:T(128)S(1)} %eq.39), kind=kOutput, calls=%fused_computation | convolution fusion | flops 261882832 | bytes 18874584 | tf_op jit(solution)/shard_map/mn,anf->maf/dot_general | solution.py:122
  75.4 19.9 %reshape.442 = bf16[2,27,2,8,8,8,128]{6,5,4,3,1,0,2:T(8,128)(2,1)} reshape(bf16[54,2,65536]{2,0,1:T(8,128)(2,1)} %convolution_convert_fusion) | data formatting | bytes 28311552 | tf_op jit(solution)/shard_map/reshape | solution.py:125
  97.0 1.0 fusion.6
  98.9 1.0 fusion.7
  100.8 1.4 fusion.8
  102.2 1.1 slice_bitcast_fusion.2
  104.1 1.0 maximum_bitcast_fusion
  108.7 2.1 convolution_bitcast_fusion
  112.3 1.1 collective-permute-done.8
  113.9 11.3 %collective-permute-done.9 = f32[110592]{0:T(1024)S(1)} collective-permute-done((f32[110592]{0:T(1024)S(1)}, f32[110592]{0:T(1024)S(1)}, u32[]{:S(2)}, u32[]{:S(2)}) %collective-permute-start.9) | collective-permute-done | bytes 442400 | tf_op jit(solution)/shard_map/ppermute | solution.py:101
  125.8 5.6 %collective-permute-done.10 = f32[55296]{0:T(1024)S(1)} collective-permute-done((f32[55296]{0:T(1024)S(1)}, f32[55296]{0:T(1024)S(1)}, u32[]{:S(2)}, u32[]{:S(2)}) %collective-permute-start.10) | collective-permute-done | bytes 221216 | tf_op jit(solution)/shard_map/ppermute | solution.py:101
  131.7 3.5 %collective-permute-done.11 = f32[27648]{0:T(1024)S(1)} collective-permute-done((f32[27648]{0:T(1024)S(1)}, f32[27648]{0:T(1024)S(1)}, u32[]{:S(2)}, u32[]{:S(2)}) %collective-permute-start.11) | collective-permute-done | bytes 110624 | tf_op jit(solution)/shard_map/ppermute | solution.py:101
  136.0 3.9 %collective-permute-done.12 = f32[13824]{0:T(1024)S(1)} collective-permute-done((f32[13824]{0:T(1024)S(1)}, f32[13824]{0:T(1024)S(1)}, u32[]{:S(2)}, u32[]{:S(2)}) %collective-permute-start.12) | collective-permute-done | bytes 55328 | tf_op jit(solution)/shard_map/ppermute | solution.py:101
  140.1 1.1 collective-permute-start.13
  141.3 3.3 %collective-permute-done.13 = f32[6912]{0:T(1024)S(1)} collective-permute-done((f32[6912]{0:T(1024)S(1)}, f32[6912]{0:T(1024)S(1)}, u32[]{:S(2)}, u32[]{:S(2)}) %collective-permute-start.13) | collective-permute-done | bytes 27680 | tf_op jit(solution)/shard_map/ppermute | solution.py:101
  144.7 1.6 collective-permute-start.14
  146.4 2.7 %collective-permute-done.14 = f32[3456]{0:T(1024)S(1)} collective-permute-done((f32[3456]{0:T(1024)S(1)}, f32[3456]{0:T(1024)S(1)}, u32[]{:S(2)}, u32[]{:S(2)}) %collective-permute-start.14) | collective-permute-done | bytes 13856 | tf_op jit(solution)/shard_map/ppermute | solution.py:101
  149.3 3.2 %collective-permute-start.15 = (f32[1728]{0:T(1024)S(1)}, f32[1728]{0:T(1024)S(1)}, u32[]{:S(2)}, u32[]{:S(2)}) collective-permute-start(f32[1728]{0:T(1024)S(1)} %dynamic_slice.63), channel_id=1, source_target_pairs={{0,4},{1,5},{2,6},{3,7},{4,0},{5,1},{6,2},{7,3},{8,12},{9,13},{10,... | collective-permute-start | bytes 20744 | tf_op jit(solution)/shard_map/ppermute | solution.py:101
  152.5 3.2 %collective-permute-done.15 = f32[1728]{0:T(1024)S(1)} collective-permute-done((f32[1728]{0:T(1024)S(1)}, f32[1728]{0:T(1024)S(1)}, u32[]{:S(2)}, u32[]{:S(2)}) %collective-permute-start.15) | collective-permute-done | bytes 6944 | tf_op jit(solution)/shard_map/ppermute | solution.py:101
  155.8 3.2 %collective-permute-start.16 = (f32[1728]{0:T(1024)S(1)}, f32[1728]{0:T(1024)S(1)}, u32[]{:S(2)}, u32[]{:S(2)}) collective-permute-start(f32[1728]{0:T(1024)S(1)} %dynamic-slice_add_fusion.7), channel_id=1, source_target_pairs={{0,4},{1,5},{2,6},{3,7},{4,0},{5,1},{6,2},{7,3},{8,12},{9,13},{10,... | collective-permute-start | bytes 20744 | tf_op jit(solution)/shard_map/ppermute | solution.py:104
  159.1 3.4 %collective-permute-done.16 = f32[1728]{0:T(1024)S(1)} collective-permute-done((f32[1728]{0:T(1024)S(1)}, f32[1728]{0:T(1024)S(1)}, u32[]{:S(2)}, u32[]{:S(2)}) %collective-permute-start.16) | collective-permute-done | bytes 6944 | tf_op jit(solution)/shard_map/ppermute | solution.py:104
  162.6 1.0 collective-permute-start.17
  163.7 3.0 %collective-permute-done.17 = f32[3456]{0:T(1024)S(1)} collective-permute-done((f32[3456]{0:T(1024)S(1)}, f32[3456]{0:T(1024)S(1)}, u32[]{:S(2)}, u32[]{:S(2)}) %collective-permute-start.17) | collective-permute-done | bytes 13856 | tf_op jit(solution)/shard_map/ppermute | solution.py:104
  166.7 0.9 collective-permute-start.18
  167.8 3.3 %collective-permute-done.18 = f32[6912]{0:T(1024)S(1)} collective-permute-done((f32[6912]{0:T(1024)S(1)}, f32[6912]{0:T(1024)S(1)}, u32[]{:S(2)}, u32[]{:S(2)}) %collective-permute-start.18) | collective-permute-done | bytes 27680 | tf_op jit(solution)/shard_map/ppermute | solution.py:104
  171.3 4.1 %collective-permute-done.19 = f32[13824]{0:T(1024)S(1)} collective-permute-done((f32[13824]{0:T(1024)S(1)}, f32[13824]{0:T(1024)S(1)}, u32[]{:S(2)}, u32[]{:S(2)}) %collective-permute-start.19) | collective-permute-done | bytes 55328 | tf_op jit(solution)/shard_map/ppermute | solution.py:104
  175.6 3.5 %collective-permute-done.20 = f32[27648]{0:T(1024)S(1)} collective-permute-done((f32[27648]{0:T(1024)S(1)}, f32[27648]{0:T(1024)S(1)}, u32[]{:S(2)}, u32[]{:S(2)}) %collective-permute-start.20) | collective-permute-done | bytes 110624 | tf_op jit(solution)/shard_map/ppermute | solution.py:104
  179.6 4.4 %collective-permute-done.21 = f32[55296]{0:T(1024)S(1)} collective-permute-done((f32[55296]{0:T(1024)S(1)}, f32[55296]{0:T(1024)S(1)}, u32[]{:S(2)}, u32[]{:S(2)}) %collective-permute-start.21) | collective-permute-done | bytes 221216 | tf_op jit(solution)/shard_map/ppermute | solution.py:104
  184.1 2.7 %convolution_convert_fusion.2 = bf16[1024,128]{1,0:T(8,128)(2,1)} fusion(bf16[1024,3456]{1,0:T(8,128)(2,1)S(1)} %bitcast.165, bf16[3456,128]{1,0:T(8,128)(2,1)S(1)} %bitcast.176), kind=kOutput, calls=%fused_computation.7 | convolution fusion | flops 906100736 | bytes 8224768 | tf_op jit(solution)/shard_map/dot_general | solution.py:136
  186.8 4.4 %collective-permute-done.22 = f32[110592]{0:T(1024)S(1)} collective-permute-done((f32[110592]{0:T(1024)S(1)}, f32[110592]{0:T(1024)S(1)}, u32[]{:S(2)}, u32[]{:S(2)}) %collective-permute-start.22) | collective-permute-done | bytes 442400 | tf_op jit(solution)/shard_map/ppermute | solution.py:104
  191.3 14.7 %collective-permute-start.23 = (f32[221184]{0:T(1024)S(1)}, f32[221184]{0:T(1024)S(1)}, u32[]{:S(2)}, u32[]{:S(2)}) collective-permute-start(f32[221184]{0:T(1024)S(1)} %maximum_select_fusion.1), channel_id=1, source_target_pairs={{0,32},{1,33},{2,34},{3,35},{4,36},{5,37},{6,38},{7,39},{8,40},{9,... | collective-permute-start | bytes 2654216 | tf_op jit(solution)/shard_map/ppermute | solution.py:104
  206.3 2.7 %convolution_convert_fusion.1 = bf16[1024,128]{1,0:T(8,128)(2,1)} fusion(bf16[1024,3456]{1,0:T(8,128)(2,1)S(1)} %bitcast.182, bf16[3456,128]{1,0:T(8,128)(2,1)S(1)} %bitcast.177), kind=kOutput, calls=%fused_computation.6 | convolution fusion | flops 906100736 | bytes 8224768 | tf_op jit(solution)/shard_map/dot_general | solution.py:137
  209.0 1.4 fusion.1
  (159 shorter events, 24.0 us)
Async XLA Ops:
  0.6 42.3 %copy-start.1 = (bf16[1,1,2,512,128]{4,3,2,1,0:T(8,128)(2,1)S(1)}, bf16[1,1,2,512,128]{4,3,2,1,0:T(8,128)(2,1)}, u32[]{:S(2)}) copy-start(bf16[1,1,2,512,128]{4,3,2,1,0:T(8,128)(2,1)} %param.20) | copy-start | bytes 786436
  0.6 42.3 %copy-start = (bf16[1,1,2,512,128]{4,3,2,1,0:T(8,128)(2,1)S(1)}, bf16[1,1,2,512,128]{4,3,2,1,0:T(8,128)(2,1)}, u32[]{:S(2)}) copy-start(bf16[1,1,2,512,128]{4,3,2,1,0:T(8,128)(2,1)} %param.21) | copy-start | bytes 786436
  1.5 31.7 %collective-permute-start = (bf16[2,2,8,128]{3,2,0,1:T(8,128)(2,1)S(1)}, bf16[2,2,8,128]{3,2,0,1:T(8,128)(2,1)S(1)}, u32[]{:S(2)}, u32[]{:S(2)}) collective-permute-start(bf16[2,2,8,128]{3,2,0,1:T(8,128)(2,1)S(1)} %bitcast.187), channel_id=1, source_target_pairs={{0,33},{1,34},{2,35},{3,36},{4,37},{5,38},{6,39},{7,40},{8,41},{9,... | collective-permute-start | bytes 24584 | tf_op jit(solution)/shard_map/ppermute | solution.py:26
  7.5 29.2 %collective-permute-start.1 = (bf16[2,2,8,8,128]{4,3,0,1,2:T(8,128)(2,1)S(1)}, bf16[2,2,8,8,128]{4,3,0,1,2:T(8,128)(2,1)S(1)}, u32[]{:S(2)}, u32[]{:S(2)}) collective-permute-start(bf16[2,2,8,8,128]{4,3,0,1,2:T(8,128)(2,1)S(1)} %bitcast.179), channel_id=1, source_target_pairs={{0,32},{32,64},{64,96},{96,128},{128,160},{160,192},{192,224},{1,3... | collective-permute-start | bytes 196616 | tf_op jit(solution)/shard_map/ppermute | solution.py:26
  9.4 31.6 %collective-permute-start.2 = (bf16[2,2,8,128]{3,2,0,1:T(8,128)(2,1)S(1)}, bf16[2,2,8,128]{3,2,0,1:T(8,128)(2,1)S(1)}, u32[]{:S(2)}, u32[]{:S(2)}) collective-permute-start(bf16[2,2,8,128]{3,2,0,1:T(8,128)(2,1)S(1)} %bitcast.186), channel_id=1, source_target_pairs={{1,32},{2,33},{3,34},{4,35},{5,36},{6,37},{7,38},{8,39},{9,40},{10... | collective-permute-start | bytes 24584 | tf_op jit(solution)/shard_map/ppermute | solution.py:26
  16.4 25.6 %collective-permute-start.3 = (bf16[2,2,8,8,128]{4,3,0,1,2:T(8,128)(2,1)S(1)}, bf16[2,2,8,8,128]{4,3,0,1,2:T(8,128)(2,1)S(1)}, u32[]{:S(2)}, u32[]{:S(2)}) collective-permute-start(bf16[2,2,8,8,128]{4,3,0,1,2:T(8,128)(2,1)S(1)} %bitcast.178), channel_id=1, source_target_pairs={{0,1},{1,2},{2,3},{3,4},{4,5},{5,6},{6,7},{7,8},{8,9},{9,10},{10,1... | collective-permute-start | bytes 196616 | tf_op jit(solution)/shard_map/ppermute | solution.py:26
  18.4 8.3 %collective-permute-start.5 = (bf16[2,2,8,128]{3,2,0,1:T(8,128)(2,1)S(1)}, bf16[2,2,8,128]{3,2,0,1:T(8,128)(2,1)S(1)}, u32[]{:S(2)}, u32[]{:S(2)}) collective-permute-start(bf16[2,2,8,128]{3,2,0,1:T(8,128)(2,1)S(1)} %bitcast.188), channel_id=1, source_target_pairs={{32,1},{33,2},{34,3},{35,4},{36,5},{37,6},{38,7},{39,8},{40,9},{41... | collective-permute-start | bytes 24584 | tf_op jit(solution)/shard_map/ppermute | solution.py:26
  26.7 17.0 %collective-permute-start.4 = (bf16[2,2,8,8,128]{4,3,0,1,2:T(8,128)(2,1)S(1)}, bf16[2,2,8,8,128]{4,3,0,1,2:T(8,128)(2,1)S(1)}, u32[]{:S(2)}, u32[]{:S(2)}) collective-permute-start(bf16[2,2,8,8,128]{4,3,0,1,2:T(8,128)(2,1)S(1)} %bitcast.181), channel_id=1, source_target_pairs={{1,0},{2,1},{3,2},{4,3},{5,4},{6,5},{7,6},{8,7},{9,8},{10,9},{11,1... | collective-permute-start | bytes 196616 | tf_op jit(solution)/shard_map/ppermute | solution.py:26
  33.2 12.3 %collective-permute-start.6 = (bf16[2,2,8,8,128]{4,3,0,1,2:T(8,128)(2,1)S(1)}, bf16[2,2,8,8,128]{4,3,0,1,2:T(8,128)(2,1)S(1)}, u32[]{:S(2)}, u32[]{:S(2)}) collective-permute-start(bf16[2,2,8,8,128]{4,3,0,1,2:T(8,128)(2,1)S(1)} %bitcast.180), channel_id=1, source_target_pairs={{32,0},{64,32},{96,64},{128,96},{160,128},{192,160},{224,192},{33,... | collective-permute-start | bytes 196616 | tf_op jit(solution)/shard_map/ppermute | solution.py:26
  36.7 9.7 %collective-permute-start.7 = (bf16[2,2,8,128]{3,2,0,1:T(8,128)(2,1)S(1)}, bf16[2,2,8,128]{3,2,0,1:T(8,128)(2,1)S(1)}, u32[]{:S(2)}, u32[]{:S(2)}) collective-permute-start(bf16[2,2,8,128]{3,2,0,1:T(8,128)(2,1)S(1)} %bitcast.189), channel_id=1, source_target_pairs={{33,0},{34,1},{35,2},{36,3},{37,4},{38,5},{39,6},{40,7},{41,8},{42... | collective-permute-start | bytes 24584 | tf_op jit(solution)/shard_map/ppermute | solution.py:26
  110.9 2.5 %collective-permute-start.8 = (f32[221184]{0:T(1024)S(1)}, f32[221184]{0:T(1024)S(1)}, u32[]{:S(2)}, u32[]{:S(2)}) collective-permute-start(f32[221184]{0:T(1024)S(1)} %dynamic_slice.49), channel_id=1, source_target_pairs={{0,32},{1,33},{2,34},{3,35},{4,36},{5,37},{6,38},{7,39},{8,40},{9,... | collective-permute-start | bytes 2654216 | tf_op jit(solution)/shard_map/ppermute | solution.py:101
  113.5 70.6 %copy-start.2 = (bf16[27,128,128]{2,1,0:T(8,128)(2,1)S(1)}, bf16[27,128,128]{2,1,0:T(8,128)(2,1)}, u32[]{:S(2)}) copy-start(bf16[27,128,128]{2,1,0:T(8,128)(2,1)} %param.22) | copy-start | bytes 2654212
  113.5 11.7 %collective-permute-start.9 = (f32[110592]{0:T(1024)S(1)}, f32[110592]{0:T(1024)S(1)}, u32[]{:S(2)}, u32[]{:S(2)}) collective-permute-start(f32[110592]{0:T(1024)S(1)} %dynamic_slice.51), channel_id=1, source_target_pairs={{0,1},{1,0},{2,3},{3,2},{4,5},{5,4},{6,7},{7,6},{8,9},{9,8},{10,11... | collective-permute-start | bytes 1327112 | tf_op jit(solution)/shard_map/ppermute | solution.py:101
  125.3 6.1 %collective-permute-start.10 = (f32[55296]{0:T(1024)S(1)}, f32[55296]{0:T(1024)S(1)}, u32[]{:S(2)}, u32[]{:S(2)}) collective-permute-start(f32[55296]{0:T(1024)S(1)} %dynamic_slice.53), channel_id=1, source_target_pairs={{0,8},{1,9},{2,10},{3,11},{4,12},{5,13},{6,14},{7,15},{8,0},{9,1},... | collective-permute-start | bytes 663560 | tf_op jit(solution)/shard_map/ppermute | solution.py:101
  131.5 3.7 %collective-permute-start.11 = (f32[27648]{0:T(1024)S(1)}, f32[27648]{0:T(1024)S(1)}, u32[]{:S(2)}, u32[]{:S(2)}) collective-permute-start(f32[27648]{0:T(1024)S(1)} %dynamic_slice.55), channel_id=1, source_target_pairs={{0,64},{1,65},{2,66},{3,67},{4,68},{5,69},{6,70},{7,71},{8,72},{9,... | collective-permute-start | bytes 331784 | tf_op jit(solution)/shard_map/ppermute | solution.py:101
  135.2 4.6 %collective-permute-start.12 = (f32[13824]{0:T(1024)S(1)}, f32[13824]{0:T(1024)S(1)}, u32[]{:S(2)}, u32[]{:S(2)}) collective-permute-start(f32[13824]{0:T(1024)S(1)} %dynamic_slice.57), channel_id=1, source_target_pairs={{0,2},{1,3},{2,0},{3,1},{4,6},{5,7},{6,4},{7,5},{8,10},{9,11},{10,... | collective-permute-start | bytes 165896 | tf_op jit(solution)/shard_map/ppermute | solution.py:101
  140.1 4.5 %collective-permute-start.13 = (f32[6912]{0:T(1024)S(1)}, f32[6912]{0:T(1024)S(1)}, u32[]{:S(2)}, u32[]{:S(2)}) collective-permute-start(f32[6912]{0:T(1024)S(1)} %dynamic_slice.59), channel_id=1, source_target_pairs={{0,16},{1,17},{2,18},{3,19},{4,20},{5,21},{6,22},{7,23},{8,24},{9,... | collective-permute-start | bytes 82952 | tf_op jit(solution)/shard_map/ppermute | solution.py:101
  144.7 4.4 %collective-permute-start.14 = (f32[3456]{0:T(1024)S(1)}, f32[3456]{0:T(1024)S(1)}, u32[]{:S(2)}, u32[]{:S(2)}) collective-permute-start(f32[3456]{0:T(1024)S(1)} %dynamic_slice.61), channel_id=1, source_target_pairs={{0,128},{1,129},{2,130},{3,131},{4,132},{5,133},{6,134},{7,135},{8... | collective-permute-start | bytes 41480 | tf_op jit(solution)/shard_map/ppermute | solution.py:101
  149.3 6.4 %collective-permute-start.15 = (f32[1728]{0:T(1024)S(1)}, f32[1728]{0:T(1024)S(1)}, u32[]{:S(2)}, u32[]{:S(2)}) collective-permute-start(f32[1728]{0:T(1024)S(1)} %dynamic_slice.63), channel_id=1, source_target_pairs={{0,4},{1,5},{2,6},{3,7},{4,0},{5,1},{6,2},{7,3},{8,12},{9,13},{10,... | collective-permute-start | bytes 20744 | tf_op jit(solution)/shard_map/ppermute | solution.py:101
  155.8 6.7 %collective-permute-start.16 = (f32[1728]{0:T(1024)S(1)}, f32[1728]{0:T(1024)S(1)}, u32[]{:S(2)}, u32[]{:S(2)}) collective-permute-start(f32[1728]{0:T(1024)S(1)} %dynamic-slice_add_fusion.7), channel_id=1, source_target_pairs={{0,4},{1,5},{2,6},{3,7},{4,0},{5,1},{6,2},{7,3},{8,12},{9,13},{10,... | collective-permute-start | bytes 20744 | tf_op jit(solution)/shard_map/ppermute | solution.py:104
  162.6 4.1 %collective-permute-start.17 = (f32[3456]{0:T(1024)S(1)}, f32[3456]{0:T(1024)S(1)}, u32[]{:S(2)}, u32[]{:S(2)}) collective-permute-start(f32[3456]{0:T(1024)S(1)} %maximum_select_fusion.7), channel_id=1, source_target_pairs={{0,128},{1,129},{2,130},{3,131},{4,132},{5,133},{6,134},{7,135},{8... | collective-permute-start | bytes 41480 | tf_op jit(solution)/shard_map/ppermute | solution.py:104
  166.7 4.3 %collective-permute-start.18 = (f32[6912]{0:T(1024)S(1)}, f32[6912]{0:T(1024)S(1)}, u32[]{:S(2)}, u32[]{:S(2)}) collective-permute-start(f32[6912]{0:T(1024)S(1)} %maximum_select_fusion.6), channel_id=1, source_target_pairs={{0,16},{1,17},{2,18},{3,19},{4,20},{5,21},{6,22},{7,23},{8,24},{9,... | collective-permute-start | bytes 82952 | tf_op jit(solution)/shard_map/ppermute | solution.py:104
  171.1 4.3 %collective-permute-start.19 = (f32[13824]{0:T(1024)S(1)}, f32[13824]{0:T(1024)S(1)}, u32[]{:S(2)}, u32[]{:S(2)}) collective-permute-start(f32[13824]{0:T(1024)S(1)} %maximum_select_fusion.5), channel_id=1, source_target_pairs={{0,2},{1,3},{2,0},{3,1},{4,6},{5,7},{6,4},{7,5},{8,10},{9,11},{10,... | collective-permute-start | bytes 165896 | tf_op jit(solution)/shard_map/ppermute | solution.py:104
  175.4 3.7 %collective-permute-start.20 = (f32[27648]{0:T(1024)S(1)}, f32[27648]{0:T(1024)S(1)}, u32[]{:S(2)}, u32[]{:S(2)}) collective-permute-start(f32[27648]{0:T(1024)S(1)} %maximum_select_fusion.4), channel_id=1, source_target_pairs={{0,64},{1,65},{2,66},{3,67},{4,68},{5,69},{6,70},{7,71},{8,72},{9,... | collective-permute-start | bytes 331784 | tf_op jit(solution)/shard_map/ppermute | solution.py:104
  179.1 4.9 %collective-permute-start.21 = (f32[55296]{0:T(1024)S(1)}, f32[55296]{0:T(1024)S(1)}, u32[]{:S(2)}, u32[]{:S(2)}) collective-permute-start(f32[55296]{0:T(1024)S(1)} %maximum_select_fusion.3), channel_id=1, source_target_pairs={{0,8},{1,9},{2,10},{3,11},{4,12},{5,13},{6,14},{7,15},{8,0},{9,1},... | collective-permute-start | bytes 663560 | tf_op jit(solution)/shard_map/ppermute | solution.py:104
  184.0 7.2 %collective-permute-start.22 = (f32[110592]{0:T(1024)S(1)}, f32[110592]{0:T(1024)S(1)}, u32[]{:S(2)}, u32[]{:S(2)}) collective-permute-start(f32[110592]{0:T(1024)S(1)} %maximum_select_fusion.2), channel_id=1, source_target_pairs={{0,1},{1,0},{2,3},{3,2},{4,5},{5,4},{6,7},{7,6},{8,9},{9,8},{10,11... | collective-permute-start | bytes 1327112 | tf_op jit(solution)/shard_map/ppermute | solution.py:104
  191.3 17.7 %collective-permute-start.23 = (f32[221184]{0:T(1024)S(1)}, f32[221184]{0:T(1024)S(1)}, u32[]{:S(2)}, u32[]{:S(2)}) collective-permute-start(f32[221184]{0:T(1024)S(1)} %maximum_select_fusion.1), channel_id=1, source_target_pairs={{0,32},{1,33},{2,34},{3,35},{4,36},{5,37},{6,38},{7,39},{8,40},{9,... | collective-permute-start | bytes 2654216 | tf_op jit(solution)/shard_map/ppermute | solution.py:104

commit v2 on v1

--- a/solution.py
+++ b/solution.py
@@ -26,24 +26,36 @@
     return lax.ppermute(x, axes if len(axes) > 1 else axes[0], pairs)
 
 
-def neighbour_pool(both):
-    x7, x0 = both[:, :, 7], both[:, :, 0]
-    y7, y0 = both[:, :, :, 7], both[:, :, :, 0]
-    zero = jnp.zeros_like(both)
+def neighbour_pool(blocks, block_edge):
+    e = block_edge
+    s, v, c = blocks.shape
+    rows = blocks.reshape(s, e, e * e, c)
+    hi, lo = (e - 1) * e, e
+    zero = jnp.zeros_like(rows)
     recv = {
-        (-1, 0): zero.at[:, :, 7].set(shift(x7, ("gx",), (1,))),
-        (1, 0): zero.at[:, :, 0].set(shift(x0, ("gx",), (-1,))),
-        (0, -1): zero.at[:, :, :, 7].set(shift(y7, ("gy",), (1,))),
-        (0, 1): zero.at[:, :, :, 0].set(shift(y0, ("gy",), (-1,))),
-        (-1, -1): zero.at[:, :, 7, 7].set(shift(both[:, :, 7, 7], ("gx", "gy"), (1, 1))),
-        (-1, 1): zero.at[:, :, 7, 0].set(shift(both[:, :, 7, 0], ("gx", "gy"), (1, -1))),
-        (1, -1): zero.at[:, :, 0, 7].set(shift(both[:, :, 0, 7], ("gx", "gy"), (-1, 1))),
-        (1, 1): zero.at[:, :, 0, 0].set(shift(both[:, :, 0, 0], ("gx", "gy"), (-1, -1))),
-        (0, 0): both,
+        (-1, 0): zero.at[:, e - 1].set(shift(rows[:, e - 1], ("gx",), (1,))),
+        (1, 0): zero.at[:, 0].set(shift(rows[:, 0], ("gx",), (-1,))),
+        (0, -1): zero.at[:, :, hi:].set(shift(rows[:, :, hi:], ("gy",), (1,))),
+        (0, 1): zero.at[:, :, :lo].set(shift(rows[:, :, :lo], ("gy",), (-1,))),
+        (-1, -1): zero.at[:, e - 1, hi:].set(shift(rows[:, e - 1, hi:], ("gx", "gy"), (1, 1))),
+        (-1, 1): zero.at[:, e - 1, :lo].set(shift(rows[:, e - 1, :lo], ("gx", "gy"), (1, -1))),
+        (1, -1): zero.at[:, 0, hi:].set(shift(rows[:, 0, hi:], ("gx", "gy"), (-1, 1))),
+        (1, 1): zero.at[:, 0, :lo].set(shift(rows[:, 0, :lo], ("gx", "gy"), (-1, -1))),
+        (0, 0): rows,
     }
-    blocks = [recv[(di, dj)] for di in (-1, 0, 1) for dj in (-1, 0, 1)]
-    pool = jnp.stack(blocks, axis=1)
-    return pool.reshape(2, 9 * both.shape[1], -1)
+    pool = jnp.concatenate([recv[(di, dj)] for di in (-1, 0, 1) for dj in (-1, 0, 1)])
+    return pool.reshape(9 * s, v, c)
+
+
+def padded_columns(blocks, ids, block_edge):
+    e = block_edge
+    s, v, c = blocks.shape
+    pool = neighbour_pool(blocks, e)
+    onehot = (ids[:, None] == jnp.arange(pool.shape[0])[None, :]).astype(pool.dtype)
+    picked = jnp.einsum("mn,nvc->mvc", onehot, pool, preferred_element_type=jnp.float32)
+    picked = picked.reshape(s, 27, e, e, e, c)
+    cube = assemble(picked, e)
+    return im2col(cube, e).astype(blocks.dtype)
 
 
 def assemble(picked, block_edge):
@@ -58,17 +70,15 @@
                 portion = picked[
                     :,
                     k,
-                    :,
                     ranges[a][0] : ranges[a][1],
                     ranges[b][0] : ranges[b][1],
                     ranges[c][0] : ranges[c][1],
                     :,
                 ]
                 columns.append(portion)
-            row_list.append(jnp.concatenate(columns, axis=4))
-        planes.append(jnp.concatenate(row_list, axis=3))
-    cube = jnp.concatenate(planes, axis=2)
-    return jnp.swapaxes(cube, 0, 1)
+            row_list.append(jnp.concatenate(columns, axis=3))
+        planes.append(jnp.concatenate(row_list, axis=2))
+    return jnp.concatenate(planes, axis=1)
 
 
 def im2col(cube, block_edge):
@@ -112,25 +122,14 @@
     slot_count = features.shape[2]
     voxels = features.shape[3]
     channels = features.shape[4]
-    e = BLK
-    both = jnp.stack([features[0, 0], grad_out[0, 0]]).reshape(
-        2, slot_count, e, e, e, channels
-    )
-    pool = neighbour_pool(both)
     ids = neighbours.reshape(slot_count * 27)
-    onehot = (ids[:, None] == jnp.arange(pool.shape[1])[None, :]).astype(pool.dtype)
-    picked = jnp.einsum(
-        "mn,anf->maf", onehot, pool, preferred_element_type=jnp.float32
-    ).astype(pool.dtype)
-    picked = picked.reshape(slot_count, 27, 2, e, e, e, channels)
-    cubes = assemble(picked, e)
-    cols_feat = im2col(cubes[0], e)
-    cols_grad = im2col(cubes[1], e)
+    cols_feat = padded_columns(features.reshape(slot_count, voxels, channels), ids, BLK)
     grad_flat = grad_out.reshape(-1, channels)
     partial_value = lax.dot_general(
         cols_feat, grad_flat, (((0,), (0,)), ((), ())), preferred_element_type=jnp.float32
     ).reshape(27, channels, channels)
     summed = butterfly_sum(partial_value, ("gx", "gy"))
+    cols_grad = padded_columns(grad_out.reshape(slot_count, voxels, channels), ids, BLK)
     w_out = weight.reshape(27 * channels, channels)
     w_in = jnp.swapaxes(weight[::-1], 1, 2).reshape(27 * channels, channels)
     output = jnp.dot(cols_feat, w_out, preferred_element_type=jnp.float32)

time: 212 us -> 226 us (1.066); the launches traced: 210 us -> 221 us
  starting transfers between devices: 54.9 us -> 78.4 us
  local copies, waits for them, and re-layouts: 57.7 us -> 47 us
  matrix products: 24 us -> 14.2 us
  waiting for transfers between devices: 62.3 us -> 71.5 us
    reshape x2 -> x0, local copies, waits for them, and re-layouts: 31.6 us -> none  [the longest x1 19.9 us: local(): picked = picked.reshape(slot_count, 27, 2, e, e, e, channels)]
    ppermute x8 -> x16, starting transfers between devices: 27.4 us -> 52.4 us  [shift(): return lax.ppermute(x, axes if len(axes) > 1 else axes[0], pairs)]
    dot_general x1 -> x2, matrix products: 16.5 us -> 6.63 us  [padded_columns(): jnp.einsum('mn,nvc->mvc', onehot, pool, preferred_element_type=jnp.float32)]
    scatter x0 -> x16, local copies, waits for them, and re-layouts: none -> 9.54 us  [the longest x2 5.24 us: neighbour_pool(): zero.at[:, 0, hi:].set(shift(rows[:, 0, hi:], ('gx', 'gy'), (-1, 1)))]
    dot_general x0 -> x2, local copies, waits for them, and re-layouts: none -> 6.54 us  [padded_columns(): jnp.einsum('mn,nvc->mvc', onehot, pool, preferred_element_type=jnp.float32)]
    ppermute x8 -> x16, waiting for transfers between devices: 1.68 us -> 6.6 us  [shift(): return lax.ppermute(x, axes if len(axes) > 1 else axes[0], pairs)]
    ppermute x8, waiting for transfers between devices: 26.1 us -> 30.8 us  [butterfly_sum(): other = lax.ppermute(flat, axes, pairs(b))]
    slice x4 -> x22, local copies, waits for them, and re-layouts: 4.24 us -> 8.6 us  [the longest x12 3.59 us: assemble(): picked[:, k, ranges[a][0]:ranges[a][1], ranges[b][0]:ranges[b][1], ranges...]
  transfers between devices with their start and end apart: 24 -> 32, of which waited for: 16 -> 16; matrix products, arithmetic and copies ran while one was open for 12% -> 21% of each run, Pallas kernels for 0% -> 0%
where the time goes in v2:
time: 226 us; the launch traced here: 221 us
  starting transfers between devices  78.4 us (35%)
  waiting for transfers between devices  71.5 us (32%)
  local copies, waits for them, and re-layouts  47 us (21%)
  matrix products  14.2 us (6%)
  other arithmetic  7.93 us (4%)
  between operations  2.4 us (1%)
    ppermute x16, starting transfers between devices, shift(): return lax.ppermute(x, axes if len(axes) > 1 else axes[0], pairs)  52.4 us
    ppermute x8, waiting for transfers between devices, butterfly_sum(): flat = keep + lax.ppermute(send, axes, pairs(b))  34.1 us
    ppermute x8, waiting for transfers between devices, butterfly_sum(): other = lax.ppermute(flat, axes, pairs(b))  30.8 us
    ppermute x8, starting transfers between devices, butterfly_sum(): other = lax.ppermute(flat, axes, pairs(b))  19 us
    unnamed x109, local copies, waits for them, and re-layouts  12.4 us
    ppermute x8, starting transfers between devices, butterfly_sum(): flat = keep + lax.ppermute(send, axes, pairs(b))  6.99 us
    dot_general x2, matrix products, padded_columns(): jnp.einsum('mn,nvc->mvc', onehot, pool, preferred_element_type=jnp.float32)  6.63 us
    ppermute x16, waiting for transfers between devices, shift(): return lax.ppermute(x, axes if len(axes) > 1 else axes[0], pairs)  6.6 us
  transfers between devices with their start and end apart: 32, of which 16 were waited for; matrix products, arithmetic and copies ran while one was open for 21% of the time, Pallas kernels for 0%

profile of v2, /device:TPU:15, one launch (start us, length us, event | category | flops | bytes accessed | tf_op | source)
XLA Modules:
  0.0 221.4 jit_solution(3217017341321487920)
XLA Ops:
  1.4 8.3 %collective-permute-start.7 = (bf16[2,8,128]{2,1,0:T(8,128)(2,1)S(1)}, bf16[2,8,128]{2,1,0:T(8,128)(2,1)S(1)}, u32[]{:S(2)}, u32[]{:S(2)}) collective-permute-start(bf16[2,8,128]{2,1,0:T(8,128)(2,1)S(1)} %get-tuple-element.313), channel_id=1, source_target_pairs={{33,0},{34,1},{35,2},{36,3},{37,4},{38,5},{39,6},{40,7},{41,8},{42... | collective-permute-start | bytes 12296 | tf_op jit(solution)/shard_map/ppermute | solution.py:26
  9.7 1.9 collective-permute-start.5
  11.6 6.7 %collective-permute-start.2 = (bf16[2,8,128]{2,1,0:T(8,128)(2,1)S(1)}, bf16[2,8,128]{2,1,0:T(8,128)(2,1)S(1)}, u32[]{:S(2)}, u32[]{:S(2)}) collective-permute-start(bf16[2,8,128]{2,1,0:T(8,128)(2,1)S(1)} %get-tuple-element.315), channel_id=1, source_target_pairs={{1,32},{2,33},{3,34},{4,35},{5,36},{6,37},{7,38},{8,39},{9,40},{10... | collective-permute-start | bytes 12296 | tf_op jit(solution)/shard_map/ppermute | solution.py:26
  18.3 1.9 collective-permute-start
  20.9 1.9 collective-permute-start.13
  22.9 1.4 slice_bitcast_fusion.4
  29.3 1.9 copy.149
  32.2 2.0 collective-permute-start.8
  34.3 5.0 %collective-permute-done.8 = bf16[2,8,128]{2,1,0:T(8,128)(2,1)S(1)} collective-permute-done((bf16[2,8,128]{2,1,0:T(8,128)(2,1)S(1)}, bf16[2,8,128]{2,1,0:T(8,128)(2,1)S(1)}, u32[]{:S(2)}, u32[]{:S(2)}) %collective-permute-start.8) | collective-permute-done | bytes 4128 | tf_op jit(solution)/shard_map/ppermute | solution.py:26
  39.4 4.5 %collective-permute-start.15 = (bf16[2,8,128]{2,1,0:T(8,128)(2,1)S(1)}, bf16[2,8,128]{2,1,0:T(8,128)(2,1)S(1)}, u32[]{:S(2)}, u32[]{:S(2)}) collective-permute-start(bf16[2,8,128]{2,1,0:T(8,128)(2,1)S(1)} %get-tuple-element.303), channel_id=1, source_target_pairs={{33,0},{34,1},{35,2},{36,3},{37,4},{38,5},{39,6},{40,7},{41,8},{42... | collective-permute-start | bytes 12296 | tf_op jit(solution)/shard_map/ppermute | solution.py:26
  44.0 3.9 %collective-permute-start.10 = (bf16[2,8,128]{2,1,0:T(8,128)(2,1)S(1)}, bf16[2,8,128]{2,1,0:T(8,128)(2,1)S(1)}, u32[]{:S(2)}, u32[]{:S(2)}) collective-permute-start(bf16[2,8,128]{2,1,0:T(8,128)(2,1)S(1)} %get-tuple-element.305), channel_id=1, source_target_pairs={{1,32},{2,33},{3,34},{4,35},{5,36},{6,37},{7,38},{8,39},{9,40},{10... | collective-permute-start | bytes 12296 | tf_op jit(solution)/shard_map/ppermute | solution.py:26
  47.8 2.6 %collective-permute-start.9 = (bf16[2,64,128]{2,1,0:T(8,128)(2,1)S(1)}, bf16[2,64,128]{2,1,0:T(8,128)(2,1)S(1)}, u32[]{:S(2)}, u32[]{:S(2)}) collective-permute-start(bf16[2,64,128]{2,1,0:T(8,128)(2,1)S(1)} %get-tuple-element.308), channel_id=1, source_target_pairs={{0,32},{32,64},{64,96},{96,128},{128,160},{160,192},{192,224},{1,3... | collective-permute-start | bytes 98312 | tf_op jit(solution)/shard_map/ppermute | solution.py:26
  51.8 1.9 collective-permute-start.6
  54.5 3.6 %collective-permute-start.1 = (bf16[2,64,128]{2,1,0:T(8,128)(2,1)}, bf16[2,64,128]{2,1,0:T(8,128)(2,1)}, u32[]{:S(2)}, u32[]{:S(2)}) collective-permute-start(bf16[2,64,128]{2,1,0:T(8,128)(2,1)} %get-tuple-element.318), channel_id=1, source_target_pairs={{0,32},{32,64},{64,96},{96,128},{128,160},{160,192},{192,224},{1,3... | collective-permute-start | bytes 98312 | tf_op jit(solution)/shard_map/ppermute | solution.py:26
  58.9 2.5 %collective-permute-start.4 = (bf16[2,8,8,128]{3,2,1,0:T(8,128)(2,1)}, bf16[2,8,8,128]{3,2,1,0:T(8,128)(2,1)}, u32[]{:S(2)}, u32[]{:S(2)}) collective-permute-start(bf16[2,8,8,128]{3,2,1,0:T(8,128)(2,1)} %get-tuple-element.319), channel_id=1, source_target_pairs={{1,0},{2,1},{3,2},{4,3},{5,4},{6,5},{7,6},{8,7},{9,8},{10,9},{11,1... | collective-permute-start | bytes 98312 | tf_op jit(solution)/shard_map/ppermute | solution.py:26
  61.4 1.9 collective-permute-start.14
  64.2 2.6 %scatter.61 = bf16[2,8,64,128]{3,2,1,0:T(8,128)(2,1)} dynamic-update-slice(bf16[2,8,64,128]{3,2,1,0:T(8,128)(2,1)} %broadcast.331.clone, bf16[2,1,8,128]{3,2,1,0:T(8,128)(2,1)S(1)} %get-tuple-element.324, s32[]{:T(128)} %constant.401.clone.1, s32[]{:T(128)} %bitcast.20, s32[]{:T(128)} %bitcast.21, s32[]{:T(128)} %constant.401.clone.1) | dynamic-update-slice | bytes 8196 | tf_op jit(solution)/shard_map/scatter | solution.py:42
  67.6 2.6 %scatter.75 = bf16[2,8,64,128]{3,2,1,0:T(8,128)(2,1)} dynamic-update-slice(bf16[2,8,64,128]{3,2,1,0:T(8,128)(2,1)} %broadcast.331.clone.1, bf16[2,1,8,128]{3,2,1,0:T(8,128)(2,1)S(1)} %get-tuple-element.323, s32[]{:T(128)} %constant.401.clone.1, s32[]{:T(128)} %bitcast.20, s32[]{:T(128)} %bitcast.21, s32[]{:T(128)} %constant.401.clone.1) | dynamic-update-slice | bytes 8196 | tf_op jit(solution)/shard_map/scatter | solution.py:42
  70.2 2.9 %collective-permute-start.11 = (bf16[2,8,8,128]{3,2,1,0:T(8,128)(2,1)S(1)}, bf16[2,8,8,128]{3,2,1,0:T(8,128)(2,1)S(1)}, u32[]{:S(2)}, u32[]{:S(2)}) collective-permute-start(bf16[2,8,8,128]{3,2,1,0:T(8,128)(2,1)S(1)} %get-tuple-element.310), channel_id=1, source_target_pairs={{0,1},{1,2},{2,3},{3,4},{4,5},{5,6},{6,7},{7,8},{8,9},{9,10},{10,1... | collective-permute-start | bytes 98312 | tf_op jit(solution)/shard_map/ppermute | solution.py:26
  73.9 1.7 constant_dynamic-update-slice_fusion.40
  75.6 1.5 collective-permute-done.11
  77.1 3.0 %collective-permute-start.12 = (bf16[2,8,8,128]{3,2,1,0:T(8,128)(2,1)S(1)}, bf16[2,8,8,128]{3,2,1,0:T(8,128)(2,1)S(1)}, u32[]{:S(2)}, u32[]{:S(2)}) collective-permute-start(bf16[2,8,8,128]{3,2,1,0:T(8,128)(2,1)S(1)} %get-tuple-element.309), channel_id=1, source_target_pairs={{1,0},{2,1},{3,2},{4,3},{5,4},{6,5},{7,6},{8,7},{9,8},{10,9},{11,1... | collective-permute-start | bytes 98312 | tf_op jit(solution)/shard_map/ppermute | solution.py:26
  81.7 2.7 %collective-permute-start.3 = (bf16[2,8,8,128]{3,2,1,0:T(8,128)(2,1)}, bf16[2,8,8,128]{3,2,1,0:T(8,128)(2,1)S(1)}, u32[]{:S(2)}, u32[]{:S(2)}) collective-permute-start(bf16[2,8,8,128]{3,2,1,0:T(8,128)(2,1)} %get-tuple-element.320), channel_id=1, source_target_pairs={{0,1},{1,2},{2,3},{3,4},{4,5},{5,6},{6,7},{7,8},{8,9},{9,10},{10,1... | collective-permute-start | bytes 98312 | tf_op jit(solution)/shard_map/ppermute | solution.py:26
  87.5 3.3 %copy.120 = bf16[512,128,18]{1,2,0:T(8,128)(2,1)S(1)} copy(bf16[512,128,18]{1,0,2:T(8,128)(2,1)} %bitcast.388) | data formatting | bytes 4718592 | tf_op jit(solution)/shard_map/mn,nvc->mvc/dot_general | solution.py:55
  90.8 2.4 %fusion.2 = f32[2,27,8,8,8,128]{5,1,4,3,2,0:T(8,128)S(1)} fusion(bf16[8,8,8,128,18,1]{3,4,2,1,0,5:T(8,128)(2,1)S(1)} %bitcast.385, s32[2,27]{1,0:T(2,128)S(1)} %bitcast.493), kind=kOutput, calls=%fused_computation.113 | convolution fusion | flops 127402960 | bytes 16515288 | tf_op jit(solution)/shard_map/mn,nvc->mvc/dot_general | solution.py:55
  99.0 3.3 %copy.85 = bf16[512,128,18]{1,2,0:T(8,128)(2,1)} copy(bf16[512,128,18]{1,0,2:T(8,128)(2,1)S(1)} %bitcast.387) | data formatting | bytes 4718592 | tf_op jit(solution)/shard_map/mn,nvc->mvc/dot_general | solution.py:55
  102.2 4.3 %fusion.4 = f32[2,27,8,8,8,128]{5,1,4,3,2,0:T(8,128)S(1)} fusion(bf16[8,8,8,128,18,1]{3,4,2,1,0,5:T(8,128)(2,1)} %bitcast.386, s32[2,27]{1,0:T(2,128)S(1)} %bitcast.494), kind=kOutput, calls=%fused_computation.114 | convolution fusion | flops 127402960 | bytes 16515288 | tf_op jit(solution)/shard_map/mn,nvc->mvc/dot_general | solution.py:55
  114.9 2.1 convolution_bitcast_fusion
  117.1 2.1 collective-permute-start.16
  122.5 10.5 %collective-permute-done.17 = f32[110592]{0:T(1024)S(1)} collective-permute-done((f32[110592]{0:T(1024)S(1)}, f32[110592]{0:T(1024)S(1)}, u32[]{:S(2)}, u32[]{:S(2)}) %collective-permute-start.17) | collective-permute-done | bytes 442400 | tf_op jit(solution)/shard_map/ppermute | solution.py:111
  133.9 5.4 %collective-permute-done.18 = f32[55296]{0:T(1024)S(1)} collective-permute-done((f32[55296]{0:T(1024)S(1)}, f32[55296]{0:T(1024)S(1)}, u32[]{:S(2)}, u32[]{:S(2)}) %collective-permute-start.18) | collective-permute-done | bytes 221216 | tf_op jit(solution)/shard_map/ppermute | solution.py:111
  139.5 3.5 %collective-permute-done.19 = f32[27648]{0:T(1024)S(1)} collective-permute-done((f32[27648]{0:T(1024)S(1)}, f32[27648]{0:T(1024)S(1)}, u32[]{:S(2)}, u32[]{:S(2)}) %collective-permute-start.19) | collective-permute-done | bytes 110624 | tf_op jit(solution)/shard_map/ppermute | solution.py:111
  144.0 3.8 %collective-permute-done.20 = f32[13824]{0:T(1024)S(1)} collective-permute-done((f32[13824]{0:T(1024)S(1)}, f32[13824]{0:T(1024)S(1)}, u32[]{:S(2)}, u32[]{:S(2)}) %collective-permute-start.20) | collective-permute-done | bytes 55328 | tf_op jit(solution)/shard_map/ppermute | solution.py:111
  148.9 3.3 %collective-permute-done.21 = f32[6912]{0:T(1024)S(1)} collective-permute-done((f32[6912]{0:T(1024)S(1)}, f32[6912]{0:T(1024)S(1)}, u32[]{:S(2)}, u32[]{:S(2)}) %collective-permute-start.21) | collective-permute-done | bytes 27680 | tf_op jit(solution)/shard_map/ppermute | solution.py:111
  152.4 2.6 %collective-permute-start.22 = (f32[3456]{0:T(1024)S(1)}, f32[3456]{0:T(1024)S(1)}, u32[]{:S(2)}, u32[]{:S(2)}) collective-permute-start(f32[3456]{0:T(1024)S(1)} %dynamic_slice.61), channel_id=1, source_target_pairs={{0,128},{1,129},{2,130},{3,131},{4,132},{5,133},{6,134},{7,135},{8... | collective-permute-start | bytes 41480 | tf_op jit(solution)/shard_map/ppermute | solution.py:111
  155.0 1.8 collective-permute-done.22
  157.6 5.8 %collective-permute-done.23 = f32[1728]{0:T(1024)S(1)} collective-permute-done((f32[1728]{0:T(1024)S(1)}, f32[1728]{0:T(1024)S(1)}, u32[]{:S(2)}, u32[]{:S(2)}) %collective-permute-start.23) | collective-permute-done | bytes 6944 | tf_op jit(solution)/shard_map/ppermute | solution.py:111
  164.1 5.8 %collective-permute-done.24 = f32[1728]{0:T(1024)S(1)} collective-permute-done((f32[1728]{0:T(1024)S(1)}, f32[1728]{0:T(1024)S(1)}, u32[]{:S(2)}, u32[]{:S(2)}) %collective-permute-start.24) | collective-permute-done | bytes 6944 | tf_op jit(solution)/shard_map/ppermute | solution.py:114
  170.0 2.3 %collective-permute-start.25 = (f32[3456]{0:T(1024)S(1)}, f32[3456]{0:T(1024)S(1)}, u32[]{:S(2)}, u32[]{:S(2)}) collective-permute-start(f32[3456]{0:T(1024)S(1)} %maximum_select_fusion.7), channel_id=1, source_target_pairs={{0,128},{1,129},{2,130},{3,131},{4,132},{5,133},{6,134},{7,135},{8... | collective-permute-start | bytes 41480 | tf_op jit(solution)/shard_map/ppermute | solution.py:114
  172.3 1.8 collective-permute-done.25
  174.8 3.6 %collective-permute-done.26 = f32[6912]{0:T(1024)S(1)} collective-permute-done((f32[6912]{0:T(1024)S(1)}, f32[6912]{0:T(1024)S(1)}, u32[]{:S(2)}, u32[]{:S(2)}) %collective-permute-start.26) | collective-permute-done | bytes 27680 | tf_op jit(solution)/shard_map/ppermute | solution.py:114
  178.6 4.7 %collective-permute-done.27 = f32[13824]{0:T(1024)S(1)} collective-permute-done((f32[13824]{0:T(1024)S(1)}, f32[13824]{0:T(1024)S(1)}, u32[]{:S(2)}, u32[]{:S(2)}) %collective-permute-start.27) | collective-permute-done | bytes 55328 | tf_op jit(solution)/shard_map/ppermute | solution.py:114
  183.7 3.4 %collective-permute-done.28 = f32[27648]{0:T(1024)S(1)} collective-permute-done((f32[27648]{0:T(1024)S(1)}, f32[27648]{0:T(1024)S(1)}, u32[]{:S(2)}, u32[]{:S(2)}) %collective-permute-start.28) | collective-permute-done | bytes 110624 | tf_op jit(solution)/shard_map/ppermute | solution.py:114
  187.3 4.6 %collective-permute-done.29 = f32[55296]{0:T(1024)S(1)} collective-permute-done((f32[55296]{0:T(1024)S(1)}, f32[55296]{0:T(1024)S(1)}, u32[]{:S(2)}, u32[]{:S(2)}) %collective-permute-start.29) | collective-permute-done | bytes 221216 | tf_op jit(solution)/shard_map/ppermute | solution.py:114
  192.4 6.9 %collective-permute-done.30 = f32[110592]{0:T(1024)S(1)} collective-permute-done((f32[110592]{0:T(1024)S(1)}, f32[110592]{0:T(1024)S(1)}, u32[]{:S(2)}, u32[]{:S(2)}) %collective-permute-start.30) | collective-permute-done | bytes 442400 | tf_op jit(solution)/shard_map/ppermute | solution.py:114
  199.3 15.0 %collective-permute-start.31 = (f32[221184]{0:T(1024)S(1)}, f32[221184]{0:T(1024)S(1)}, u32[]{:S(2)}, u32[]{:S(2)}) collective-permute-start(f32[221184]{0:T(1024)S(1)} %maximum_select_fusion.1), channel_id=1, source_target_pairs={{0,32},{1,33},{2,34},{3,35},{4,36},{5,37},{6,38},{7,39},{8,40},{9,... | collective-permute-start | bytes 2654216 | tf_op jit(solution)/shard_map/ppermute | solution.py:114
  214.3 2.7 %convolution_convert_fusion.1 = bf16[1024,128]{1,0:T(8,128)(2,1)} fusion(bf16[1024,3456]{1,0:T(8,128)(2,1)S(1)} %constant_dynamic-update-slice_fusion.8, bf16[3456,128]{1,0:T(8,128)(2,1)S(1)} %bitcast.470), kind=kOutput, calls=%fused_computation.8 | convolution fusion | flops 906100736 | bytes 8224768 | tf_op jit(solution)/shard_map/dot_general | solution.py:135
  217.0 2.7 %convolution_convert_fusion = bf16[1024,128]{1,0:T(8,128)(2,1)} fusion(bf16[1024,3456]{1,0:T(8,128)(2,1)S(1)} %constant_dynamic-update-slice_fusion.43, bf16[3456,128]{1,0:T(8,128)(2,1)S(1)} %bitcast.471), kind=kOutput, calls=%fused_computation.7 | convolution fusion | flops 906100736 | bytes 8224768 | tf_op jit(solution)/shard_map/dot_general | solution.py:136
  (237 shorter events, 42.3 us)
Async XLA Ops:
  1.4 60.1 %collective-permute-start.7 = (bf16[2,8,128]{2,1,0:T(8,128)(2,1)S(1)}, bf16[2,8,128]{2,1,0:T(8,128)(2,1)S(1)}, u32[]{:S(2)}, u32[]{:S(2)}) collective-permute-start(bf16[2,8,128]{2,1,0:T(8,128)(2,1)S(1)} %get-tuple-element.313), channel_id=1, source_target_pairs={{33,0},{34,1},{35,2},{36,3},{37,4},{38,5},{39,6},{40,7},{41,8},{42... | collective-permute-start | bytes 12296 | tf_op jit(solution)/shard_map/ppermute | solution.py:26
  9.7 34.3 %collective-permute-start.5 = (bf16[2,8,128]{2,1,0:T(8,128)(2,1)S(1)}, bf16[2,8,128]{2,1,0:T(8,128)(2,1)S(1)}, u32[]{:S(2)}, u32[]{:S(2)}) collective-permute-start(bf16[2,8,128]{2,1,0:T(8,128)(2,1)S(1)} %get-tuple-element.314), channel_id=1, source_target_pairs={{32,1},{33,2},{34,3},{35,4},{36,5},{37,6},{38,7},{39,8},{40,9},{41... | collective-permute-start | bytes 12296 | tf_op jit(solution)/shard_map/ppermute | solution.py:26
  11.6 47.3 %collective-permute-start.2 = (bf16[2,8,128]{2,1,0:T(8,128)(2,1)S(1)}, bf16[2,8,128]{2,1,0:T(8,128)(2,1)S(1)}, u32[]{:S(2)}, u32[]{:S(2)}) collective-permute-start(bf16[2,8,128]{2,1,0:T(8,128)(2,1)S(1)} %get-tuple-element.315), channel_id=1, source_target_pairs={{1,32},{2,33},{3,34},{4,35},{5,36},{6,37},{7,38},{8,39},{9,40},{10... | collective-permute-start | bytes 12296 | tf_op jit(solution)/shard_map/ppermute | solution.py:26
  18.3 13.9 %collective-permute-start = (bf16[2,8,128]{2,1,0:T(8,128)(2,1)S(1)}, bf16[2,8,128]{2,1,0:T(8,128)(2,1)S(1)}, u32[]{:S(2)}, u32[]{:S(2)}) collective-permute-start(bf16[2,8,128]{2,1,0:T(8,128)(2,1)S(1)} %get-tuple-element.316), channel_id=1, source_target_pairs={{0,33},{1,34},{2,35},{3,36},{4,37},{5,38},{6,39},{7,40},{8,41},{9,... | collective-permute-start | bytes 12296 | tf_op jit(solution)/shard_map/ppermute | solution.py:26
  20.9 26.9 %collective-permute-start.13 = (bf16[2,8,128]{2,1,0:T(8,128)(2,1)S(1)}, bf16[2,8,128]{2,1,0:T(8,128)(2,1)S(1)}, u32[]{:S(2)}, u32[]{:S(2)}) collective-permute-start(bf16[2,8,128]{2,1,0:T(8,128)(2,1)S(1)} %get-tuple-element.304), channel_id=1, source_target_pairs={{32,1},{33,2},{34,3},{35,4},{36,5},{37,6},{38,7},{39,8},{40,9},{41... | collective-permute-start | bytes 12296 | tf_op jit(solution)/shard_map/ppermute | solution.py:26
  32.2 48.8 %copy-start = (bf16[1,1,2,512,128]{4,3,2,1,0:T(8,128)(2,1)S(1)}, bf16[1,1,2,512,128]{4,3,2,1,0:T(8,128)(2,1)}, u32[]{:S(2)}) copy-start(bf16[1,1,2,512,128]{4,3,2,1,0:T(8,128)(2,1)} %param.37) | copy-start | bytes 786436
  32.2 7.2 %collective-permute-start.8 = (bf16[2,8,128]{2,1,0:T(8,128)(2,1)S(1)}, bf16[2,8,128]{2,1,0:T(8,128)(2,1)S(1)}, u32[]{:S(2)}, u32[]{:S(2)}) collective-permute-start(bf16[2,8,128]{2,1,0:T(8,128)(2,1)S(1)} %get-tuple-element.306), channel_id=1, source_target_pairs={{0,33},{1,34},{2,35},{3,36},{4,37},{5,38},{6,39},{7,40},{8,41},{9,... | collective-permute-start | bytes 12296 | tf_op jit(solution)/shard_map/ppermute | solution.py:26
  39.4 15.1 %collective-permute-start.15 = (bf16[2,8,128]{2,1,0:T(8,128)(2,1)S(1)}, bf16[2,8,128]{2,1,0:T(8,128)(2,1)S(1)}, u32[]{:S(2)}, u32[]{:S(2)}) collective-permute-start(bf16[2,8,128]{2,1,0:T(8,128)(2,1)S(1)} %get-tuple-element.303), channel_id=1, source_target_pairs={{33,0},{34,1},{35,2},{36,3},{37,4},{38,5},{39,6},{40,7},{41,8},{42... | collective-permute-start | bytes 12296 | tf_op jit(solution)/shard_map/ppermute | solution.py:26
  44.0 7.9 %collective-permute-start.10 = (bf16[2,8,128]{2,1,0:T(8,128)(2,1)S(1)}, bf16[2,8,128]{2,1,0:T(8,128)(2,1)S(1)}, u32[]{:S(2)}, u32[]{:S(2)}) collective-permute-start(bf16[2,8,128]{2,1,0:T(8,128)(2,1)S(1)} %get-tuple-element.305), channel_id=1, source_target_pairs={{1,32},{2,33},{3,34},{4,35},{5,36},{6,37},{7,38},{8,39},{9,40},{10... | collective-permute-start | bytes 12296 | tf_op jit(solution)/shard_map/ppermute | solution.py:26
  47.8 22.4 %collective-permute-start.9 = (bf16[2,64,128]{2,1,0:T(8,128)(2,1)S(1)}, bf16[2,64,128]{2,1,0:T(8,128)(2,1)S(1)}, u32[]{:S(2)}, u32[]{:S(2)}) collective-permute-start(bf16[2,64,128]{2,1,0:T(8,128)(2,1)S(1)} %get-tuple-element.308), channel_id=1, source_target_pairs={{0,32},{32,64},{64,96},{96,128},{128,160},{160,192},{192,224},{1,3... | collective-permute-start | bytes 98312 | tf_op jit(solution)/shard_map/ppermute | solution.py:26
  51.8 45.3 %collective-permute-start.6 = (bf16[2,64,128]{2,1,0:T(8,128)(2,1)}, bf16[2,64,128]{2,1,0:T(8,128)(2,1)}, u32[]{:S(2)}, u32[]{:S(2)}) collective-permute-start(bf16[2,64,128]{2,1,0:T(8,128)(2,1)} %get-tuple-element.317), channel_id=1, source_target_pairs={{32,0},{64,32},{96,64},{128,96},{160,128},{192,160},{224,192},{33,... | collective-permute-start | bytes 98312 | tf_op jit(solution)/shard_map/ppermute | solution.py:26
  54.5 40.9 %collective-permute-start.1 = (bf16[2,64,128]{2,1,0:T(8,128)(2,1)}, bf16[2,64,128]{2,1,0:T(8,128)(2,1)}, u32[]{:S(2)}, u32[]{:S(2)}) collective-permute-start(bf16[2,64,128]{2,1,0:T(8,128)(2,1)} %get-tuple-element.318), channel_id=1, source_target_pairs={{0,32},{32,64},{64,96},{96,128},{128,160},{160,192},{192,224},{1,3... | collective-permute-start | bytes 98312 | tf_op jit(solution)/shard_map/ppermute | solution.py:26
  58.9 39.0 %collective-permute-start.4 = (bf16[2,8,8,128]{3,2,1,0:T(8,128)(2,1)}, bf16[2,8,8,128]{3,2,1,0:T(8,128)(2,1)}, u32[]{:S(2)}, u32[]{:S(2)}) collective-permute-start(bf16[2,8,8,128]{3,2,1,0:T(8,128)(2,1)} %get-tuple-element.319), channel_id=1, source_target_pairs={{1,0},{2,1},{3,2},{4,3},{5,4},{6,5},{7,6},{8,7},{9,8},{10,9},{11,1... | collective-permute-start | bytes 98312 | tf_op jit(solution)/shard_map/ppermute | solution.py:26
  61.4 20.2 %collective-permute-start.14 = (bf16[2,64,128]{2,1,0:T(8,128)(2,1)S(1)}, bf16[2,64,128]{2,1,0:T(8,128)(2,1)S(1)}, u32[]{:S(2)}, u32[]{:S(2)}) collective-permute-start(bf16[2,64,128]{2,1,0:T(8,128)(2,1)S(1)} %get-tuple-element.307), channel_id=1, source_target_pairs={{32,0},{64,32},{96,64},{128,96},{160,128},{192,160},{224,192},{33,... | collective-permute-start | bytes 98312 | tf_op jit(solution)/shard_map/ppermute | solution.py:26
  70.2 15.1 %copy-start.2 = (bf16[2,8,64,128]{3,2,1,0:T(8,128)(2,1)S(1)}, bf16[2,8,64,128]{3,2,1,0:T(8,128)(2,1)}, u32[]{:S(2)}) copy-start(bf16[2,8,64,128]{3,2,1,0:T(8,128)(2,1)} %scatter.75) | copy-start | bytes 786436
  70.2 16.5 %copy-start.1 = (bf16[2,8,64,128]{3,2,1,0:T(8,128)(2,1)S(1)}, bf16[2,8,64,128]{3,2,1,0:T(8,128)(2,1)}, u32[]{:S(2)}) copy-start(bf16[2,8,64,128]{3,2,1,0:T(8,128)(2,1)} %scatter.79.clone) | copy-start | bytes 786436
  70.2 6.9 %collective-permute-start.11 = (bf16[2,8,8,128]{3,2,1,0:T(8,128)(2,1)S(1)}, bf16[2,8,8,128]{3,2,1,0:T(8,128)(2,1)S(1)}, u32[]{:S(2)}, u32[]{:S(2)}) collective-permute-start(bf16[2,8,8,128]{3,2,1,0:T(8,128)(2,1)S(1)} %get-tuple-element.310), channel_id=1, source_target_pairs={{0,1},{1,2},{2,3},{3,4},{4,5},{5,6},{6,7},{7,8},{8,9},{9,10},{10,1... | collective-permute-start | bytes 98312 | tf_op jit(solution)/shard_map/ppermute | solution.py:26
  77.1 7.4 %collective-permute-start.12 = (bf16[2,8,8,128]{3,2,1,0:T(8,128)(2,1)S(1)}, bf16[2,8,8,128]{3,2,1,0:T(8,128)(2,1)S(1)}, u32[]{:S(2)}, u32[]{:S(2)}) collective-permute-start(bf16[2,8,8,128]{3,2,1,0:T(8,128)(2,1)S(1)} %get-tuple-element.309), channel_id=1, source_target_pairs={{1,0},{2,1},{3,2},{4,3},{5,4},{6,5},{7,6},{8,7},{9,8},{10,9},{11,1... | collective-permute-start | bytes 98312 | tf_op jit(solution)/shard_map/ppermute | solution.py:26
  81.7 14.7 %collective-permute-start.3 = (bf16[2,8,8,128]{3,2,1,0:T(8,128)(2,1)}, bf16[2,8,8,128]{3,2,1,0:T(8,128)(2,1)S(1)}, u32[]{:S(2)}, u32[]{:S(2)}) collective-permute-start(bf16[2,8,8,128]{3,2,1,0:T(8,128)(2,1)} %get-tuple-element.320), channel_id=1, source_target_pairs={{0,1},{1,2},{2,3},{3,4},{4,5},{5,6},{6,7},{7,8},{8,9},{9,10},{10,1... | collective-permute-start | bytes 98312 | tf_op jit(solution)/shard_map/ppermute | solution.py:26
  86.7 4.0 %copy-start.17 = (s32[1,1,2,27]{3,2,1,0:T(2,128)S(1)}, s32[1,1,2,27]{3,2,1,0:T(2,128)}, u32[]{:S(2)}) copy-start(s32[1,1,2,27]{3,2,1,0:T(2,128)} %param.39) | copy-start | bytes 652
  93.1 3.3 %copy-start.6 = (bf16[1,1,2,512,128]{4,3,2,1,0:T(8,128)(2,1)S(1)}, bf16[1,1,2,512,128]{4,3,2,1,0:T(8,128)(2,1)}, u32[]{:S(2)}) copy-start(bf16[1,1,2,512,128]{4,3,2,1,0:T(8,128)(2,1)} %param.36) | copy-start | bytes 786436
  93.1 5.7 %copy-start.3 = (bf16[2,8,64,128]{3,2,1,0:T(8,128)(2,1)S(1)}, bf16[2,8,64,128]{3,2,1,0:T(8,128)(2,1)}, u32[]{:S(2)}) copy-start(bf16[2,8,64,128]{3,2,1,0:T(8,128)(2,1)} %scatter.61) | copy-start | bytes 786436
  98.9 3.3 %copy-start.18 = (s32[1,1,2,27]{3,2,1,0:T(2,128)S(1)}, s32[1,1,2,27]{3,2,1,0:T(2,128)}, u32[]{:S(2)}) copy-start(s32[1,1,2,27]{3,2,1,0:T(2,128)} %param.39) | copy-start | bytes 652
  106.5 1.8 copy-start.14
  106.5 1.8 copy-start.15
  106.5 1.9 copy-start.7
  106.5 1.9 copy-start.8
  106.5 1.9 copy-start.9
  106.5 1.9 copy-start.10
  117.0 2.7 %copy-start.16 = (f32[2,1,1,1,8,128]{5,1,4,3,2,0:T(1,128)S(1)}, f32[2,1,1,1,8,128]{5,1,4,3,2,0:T(1,128)}, u32[]{:S(2)}) copy-start(f32[2,1,1,1,8,128]{5,1,4,3,2,0:T(1,128)} %get-tuple-element.206) | copy-start | bytes 24580
  117.1 4.3 %collective-permute-start.16 = (f32[221184]{0:T(1024)S(1)}, f32[221184]{0:T(1024)S(1)}, u32[]{:S(2)}, u32[]{:S(2)}) collective-permute-start(f32[221184]{0:T(1024)S(1)} %dynamic_slice.49), channel_id=1, source_target_pairs={{0,32},{1,33},{2,34},{3,35},{4,36},{5,37},{6,38},{7,39},{8,40},{9,... | collective-permute-start | bytes 2654216 | tf_op jit(solution)/shard_map/ppermute | solution.py:111
  121.5 11.5 %collective-permute-start.17 = (f32[110592]{0:T(1024)S(1)}, f32[110592]{0:T(1024)S(1)}, u32[]{:S(2)}, u32[]{:S(2)}) collective-permute-start(f32[110592]{0:T(1024)S(1)} %dynamic_slice.51), channel_id=1, source_target_pairs={{0,1},{1,0},{2,3},{3,2},{4,5},{5,4},{6,7},{7,6},{8,9},{9,8},{10,11... | collective-permute-start | bytes 1327112 | tf_op jit(solution)/shard_map/ppermute | solution.py:111
  133.1 6.2 %collective-permute-start.18 = (f32[55296]{0:T(1024)S(1)}, f32[55296]{0:T(1024)S(1)}, u32[]{:S(2)}, u32[]{:S(2)}) collective-permute-start(f32[55296]{0:T(1024)S(1)} %dynamic_slice.53), channel_id=1, source_target_pairs={{0,8},{1,9},{2,10},{3,11},{4,12},{5,13},{6,14},{7,15},{8,0},{9,1},... | collective-permute-start | bytes 663560 | tf_op jit(solution)/shard_map/ppermute | solution.py:111
  139.3 3.7 %collective-permute-start.19 = (f32[27648]{0:T(1024)S(1)}, f32[27648]{0:T(1024)S(1)}, u32[]{:S(2)}, u32[]{:S(2)}) collective-permute-start(f32[27648]{0:T(1024)S(1)} %dynamic_slice.55), channel_id=1, source_target_pairs={{0,64},{1,65},{2,66},{3,67},{4,68},{5,69},{6,70},{7,71},{8,72},{9,... | collective-permute-start | bytes 331784 | tf_op jit(solution)/shard_map/ppermute | solution.py:111
  143.1 4.6 %collective-permute-start.20 = (f32[13824]{0:T(1024)S(1)}, f32[13824]{0:T(1024)S(1)}, u32[]{:S(2)}, u32[]{:S(2)}) collective-permute-start(f32[13824]{0:T(1024)S(1)} %dynamic_slice.57), channel_id=1, source_target_pairs={{0,2},{1,3},{2,0},{3,1},{4,6},{5,7},{6,4},{7,5},{8,10},{9,11},{10,... | collective-permute-start | bytes 165896 | tf_op jit(solution)/shard_map/ppermute | solution.py:111
  147.9 4.3 %collective-permute-start.21 = (f32[6912]{0:T(1024)S(1)}, f32[6912]{0:T(1024)S(1)}, u32[]{:S(2)}, u32[]{:S(2)}) collective-permute-start(f32[6912]{0:T(1024)S(1)} %dynamic_slice.59), channel_id=1, source_target_pairs={{0,16},{1,17},{2,18},{3,19},{4,20},{5,21},{6,22},{7,23},{8,24},{9,... | collective-permute-start | bytes 82952 | tf_op jit(solution)/shard_map/ppermute | solution.py:111
  152.4 4.4 %collective-permute-start.22 = (f32[3456]{0:T(1024)S(1)}, f32[3456]{0:T(1024)S(1)}, u32[]{:S(2)}, u32[]{:S(2)}) collective-permute-start(f32[3456]{0:T(1024)S(1)} %dynamic_slice.61), channel_id=1, source_target_pairs={{0,128},{1,129},{2,130},{3,131},{4,132},{5,133},{6,134},{7,135},{8... | collective-permute-start | bytes 41480 | tf_op jit(solution)/shard_map/ppermute | solution.py:111
  156.9 6.4 %collective-permute-start.23 = (f32[1728]{0:T(1024)S(1)}, f32[1728]{0:T(1024)S(1)}, u32[]{:S(2)}, u32[]{:S(2)}) collective-permute-start(f32[1728]{0:T(1024)S(1)} %dynamic_slice.63), channel_id=1, source_target_pairs={{0,4},{1,5},{2,6},{3,7},{4,0},{5,1},{6,2},{7,3},{8,12},{9,13},{10,... | collective-permute-start | bytes 20744 | tf_op jit(solution)/shard_map/ppermute | solution.py:111
  163.4 6.4 %collective-permute-start.24 = (f32[1728]{0:T(1024)S(1)}, f32[1728]{0:T(1024)S(1)}, u32[]{:S(2)}, u32[]{:S(2)}) collective-permute-start(f32[1728]{0:T(1024)S(1)} %dynamic-slice_add_fusion.7), channel_id=1, source_target_pairs={{0,4},{1,5},{2,6},{3,7},{4,0},{5,1},{6,2},{7,3},{8,12},{9,13},{10,... | collective-permute-start | bytes 20744 | tf_op jit(solution)/shard_map/ppermute | solution.py:114
  170.0 4.1 %collective-permute-start.25 = (f32[3456]{0:T(1024)S(1)}, f32[3456]{0:T(1024)S(1)}, u32[]{:S(2)}, u32[]{:S(2)}) collective-permute-start(f32[3456]{0:T(1024)S(1)} %maximum_select_fusion.7), channel_id=1, source_target_pairs={{0,128},{1,129},{2,130},{3,131},{4,132},{5,133},{6,134},{7,135},{8... | collective-permute-start | bytes 41480 | tf_op jit(solution)/shard_map/ppermute | solution.py:114
  174.1 4.3 %collective-permute-start.26 = (f32[6912]{0:T(1024)S(1)}, f32[6912]{0:T(1024)S(1)}, u32[]{:S(2)}, u32[]{:S(2)}) collective-permute-start(f32[6912]{0:T(1024)S(1)} %maximum_select_fusion.6), channel_id=1, source_target_pairs={{0,16},{1,17},{2,18},{3,19},{4,20},{5,21},{6,22},{7,23},{8,24},{9,... | collective-permute-start | bytes 82952 | tf_op jit(solution)/shard_map/ppermute | solution.py:114
  178.4 4.9 %collective-permute-start.27 = (f32[13824]{0:T(1024)S(1)}, f32[13824]{0:T(1024)S(1)}, u32[]{:S(2)}, u32[]{:S(2)}) collective-permute-start(f32[13824]{0:T(1024)S(1)} %maximum_select_fusion.5), channel_id=1, source_target_pairs={{0,2},{1,3},{2,0},{3,1},{4,6},{5,7},{6,4},{7,5},{8,10},{9,11},{10,... | collective-permute-start | bytes 165896 | tf_op jit(solution)/shard_map/ppermute | solution.py:114
  183.4 3.7 %collective-permute-start.28 = (f32[27648]{0:T(1024)S(1)}, f32[27648]{0:T(1024)S(1)}, u32[]{:S(2)}, u32[]{:S(2)}) collective-permute-start(f32[27648]{0:T(1024)S(1)} %maximum_select_fusion.4), channel_id=1, source_target_pairs={{0,64},{1,65},{2,66},{3,67},{4,68},{5,69},{6,70},{7,71},{8,72},{9,... | collective-permute-start | bytes 331784 | tf_op jit(solution)/shard_map/ppermute | solution.py:114
  183.7 30.6 %copy-start.4 = (bf16[27,128,128]{2,1,0:T(8,128)(2,1)S(1)}, bf16[27,128,128]{2,1,0:T(8,128)(2,1)}, u32[]{:S(2)}) copy-start(bf16[27,128,128]{2,1,0:T(8,128)(2,1)} %param.38) | copy-start | bytes 2654212
  187.1 4.9 %collective-permute-start.29 = (f32[55296]{0:T(1024)S(1)}, f32[55296]{0:T(1024)S(1)}, u32[]{:S(2)}, u32[]{:S(2)}) collective-permute-start(f32[55296]{0:T(1024)S(1)} %maximum_select_fusion.3), channel_id=1, source_target_pairs={{0,8},{1,9},{2,10},{3,11},{4,12},{5,13},{6,14},{7,15},{8,0},{9,1},... | collective-permute-start | bytes 663560 | tf_op jit(solution)/shard_map/ppermute | solution.py:114
  192.0 7.2 %collective-permute-start.30 = (f32[110592]{0:T(1024)S(1)}, f32[110592]{0:T(1024)S(1)}, u32[]{:S(2)}, u32[]{:S(2)}) collective-permute-start(f32[110592]{0:T(1024)S(1)} %maximum_select_fusion.2), channel_id=1, source_target_pairs={{0,1},{1,0},{2,3},{3,2},{4,5},{5,4},{6,7},{7,6},{8,9},{9,8},{10,11... | collective-permute-start | bytes 1327112 | tf_op jit(solution)/shard_map/ppermute | solution.py:114
  199.3 20.4 %collective-permute-start.31 = (f32[221184]{0:T(1024)S(1)}, f32[221184]{0:T(1024)S(1)}, u32[]{:S(2)}, u32[]{:S(2)}) collective-permute-start(f32[221184]{0:T(1024)S(1)} %maximum_select_fusion.1), channel_id=1, source_target_pairs={{0,32},{1,33},{2,34},{3,35},{4,36},{5,37},{6,38},{7,39},{8,40},{9,... | collective-permute-start | bytes 2654216 | tf_op jit(solution)/shard_map/ppermute | solution.py:114
  214.3 2.7 %copy-start.5 = (bf16[27,128,128]{1,2,0:T(8,128)(2,1)S(1)}, bf16[27,128,128]{1,2,0:T(8,128)(2,1)}, u32[]{:S(2)}) copy-start(bf16[27,128,128]{1,2,0:T(8,128)(2,1)} %rev.3) | copy-start | bytes 2654212
  (3 other events, 2.2 us)
